TPU v7x, 256 devices: a whole 4x4x8 slice. The times are simulated.
256 devices in a mesh: grp: 8 (over x_hi, y), tile: 32 (over x_lo, z, core).
Axes of the slice: x: 4 (x_hi: 2, x_lo: 2; x = x_hi * 2 + x_lo), y: 4, z: 8, core: 2. Of those that a mesh axis runs over, the one named last changes fastest.
Arguments:
- tracers: float32 [64, 9, 768, 128], P('grp', None, 'tile'), may hold values from -6 to 6
- wind_x: float32 [2, 9, 32, 24, 128], P(None, None, 'tile', 'grp'), may hold values from -0.5 to 0.5, as said below
- wind_y: float32 [2, 9, 32, 24, 128], P(None, None, 'tile', 'grp'), may hold values from -0.1 to 0.1
- surface_p: float32 [2, 32, 24, 128], P(None, 'tile', 'grp'), may hold values from 0.8 to 1.2
- coef_a: float32 [9], replicated, may hold values from 0.8 to 1.2
- coef_b: float32 [9], replicated, may hold values from 0.3 to 0.7
- edge_flip: int32 [32], replicated, may hold values from 0 to 1
Outputs:
- tracers_out: float32 [64, 9, 768, 128], P('grp', None, 'tile')
- air_mass: float32 [9, 768, 128], P(None, 'tile')
Inputs may be any that keep to these rules, and one draw needn't show every extreme that they name: `edge_flip`: one entry for each edge of the cycle of tiles. `wind_x`: within each step and level all entries have the same sign, and their magnitudes lie between 0.25 and 0.5.
All inputs are finite; a program needn't handle non-finite values.
Results may differ from a plain program's by a relative error of at most 0.0003.
Values sent between devices are 32-bit elements; how exact they have to be, the bound alone decides.
No kernel may reach another device: no remote copies, remote signals or barrier semaphores. Data moves between devices by JAX's collectives and lax.ppermute only.
A program may use at most 64 MiB of HBM per device.

v0:
```python
import functools

import jax
import jax.numpy as jnp
from jax import lax
from jax.experimental import pallas as pl
from jax.experimental.pallas import tpu as pltpu
from jax.sharding import PartitionSpec as P

SECTION_WEIGHTS = (1.0 / 3.0, 0.5, 1.0)
VMEM_LIMIT = 48 * 1024 * 1024


def ring(count, step):
    return [(i, (i + step) % count) for i in range(count)]


def advect_kernel(
    dims,
    sign_ref,
    flip_ref,
    gain_a_ref,
    gain_b_ref,
    own_ref,
    low_ref,
    high_ref,
    met_own_ref,
    met_low_ref,
    met_high_ref,
    out_ref,
    mass_ref,
    q_a,
    q_b,
    q_c,
    start_ref,
    flux_x_ref,
    band_ref,
    inverse_ref,
    mass_row_ref,
):
    steps, levels, cells, block, groups, tracers, stride = dims
    width = 128
    tiles = lax.axis_size("tile")
    here = lax.axis_index("tile")
    low_flip = flip_ref[lax.rem(here + tiles - 1, tiles)]
    high_flip = flip_ref[here]

    lane = lax.broadcasted_iota(jnp.int32, (8, width), 1)
    row = lax.broadcasted_iota(jnp.int32, (8, width), 0)
    first_row = row == 0
    last_row = row == groups - 1

    def order_of(flip):
        return jnp.where(flip == 1, width - 1 - lane, lane)

    low_order = order_of(low_flip)
    high_order = order_of(high_flip)
    low_sign = jnp.where(low_flip == 1, -1.0, 1.0).astype(jnp.float32)
    high_sign = jnp.where(high_flip == 1, -1.0, 1.0).astype(jnp.float32)

    def turned(values, order):
        return jnp.take_along_axis(values, order, axis=1)

    def shift(values, by):
        return pltpu.roll(values, by % width, 1)

    def coefficients(level):
        gain_a = gain_a_ref[level]
        gain_b = gain_b_ref[level]
        refs = (met_low_ref, met_own_ref, met_high_ref)
        orders = (low_order, None, high_order)
        signs = (low_sign, None, high_sign)
        mass = None
        pressures = [
            [
                [refs[t][pl.ds(2 * steps * levels * block + s * block + c, 8, stride=stride), :] for c in range(block)]
                for t in range(3)
            ]
            for s in range(steps)
        ]
        for s in range(steps):
            flux_x = [[None] * block for _ in range(3)]
            flux_y = [[None] * block for _ in range(3)]
            start = [[None] * block for _ in range(3)]
            for t in range(3):
                for c in range(block):
                    at = s * levels * block + level * block + c
                    met = gain_a + gain_b * pressures[s][t][c]
                    x = refs[t][pl.ds(at, 8, stride=stride), :] * met
                    y = refs[t][pl.ds(steps * levels * block + at, 8, stride=stride), :] * met
                    if orders[t] is not None:
                        x = turned(x, orders[t])
                        y = turned(y, orders[t]) * signs[t]
                        if s == 0:
                            met = turned(met, orders[t])
                    flux_x[t][c] = x
                    flux_y[t][c] = y
                    if s == 0:
                        start[t][c] = met
            if s == 0:
                mass = start
            face_x = [[None] * block for _ in range(3)]
            for t in range(3):
                for c in range(block):
                    if c:
                        before = flux_x[t][c - 1]
                    else:
                        before = pltpu.roll(flux_x[t][block - 1], 1, 0)
                        if t:
                            before = jnp.where(first_row, pltpu.roll(flux_x[t - 1][block - 1], 1, 0), before)
                    face_x[t][c] = 0.5 * (before + flux_x[t][c])
            for t in range(3):
                for c in range(block):
                    if c < block - 1:
                        after = face_x[t][c + 1]
                    else:
                        after = pltpu.roll(face_x[t][0], groups - 1, 0)
                        if t < 2:
                            after = jnp.where(last_row, pltpu.roll(face_x[t + 1][0], groups - 1, 0), after)
                    face_y = jnp.where(lane == 0, 0.0, 0.5 * (shift(flux_y[t][c], 1) + flux_y[t][c]))
                    div = (after - face_x[t][c]) + (shift(face_y, -1) - face_y)
                    rows = pl.ds(t * cells + c, 8, stride=block)
                    flux_x_ref[s, rows, :] = face_x[t][c] * (1.0 / 30.0)
                    scaled = face_y * (1.0 / 30.0)
                    up = jnp.maximum(scaled, 0.0)
                    down = jnp.minimum(scaled, 0.0)
                    k0 = up
                    k1 = -6.5 * up - 1.5 * down
                    k2 = 23.5 * up + 13.5 * down
                    k3 = 13.5 * up + 23.5 * down
                    k4 = -1.5 * up - 6.5 * down
                    k5 = down
                    k2 = jnp.where(lane == 1, k2 + k1 + k0, k2)
                    k1 = jnp.where(lane == 1, 0.0, jnp.where(lane == 2, k1 + k0, k1))
                    k0 = jnp.where(lane <= 2, 0.0, k0)
                    k3 = jnp.where(lane == width - 1, k3 + k4 + k5, k3)
                    k4 = jnp.where(lane == width - 1, 0.0, jnp.where(lane == width - 2, k4 + k5, k4))
                    k5 = jnp.where(lane >= width - 2, 0.0, k5)
                    for index, value in enumerate((k0, k1, k2, k3, k4, k5)):
                        band_ref[s, index, rows, :] = value
                    mass_row_ref[s, rows, :] = mass[t][c]
                    for index, weight in enumerate(SECTION_WEIGHTS):
                        after_mass = mass[t][c] - weight * div
                        inverse_ref[s, index, rows, :] = weight / after_mass
                    mass[t][c] = mass[t][c] - div
        for c in range(block):
            mass_ref[pl.ds(level * cells + c, 8, stride=block), :] = mass[1][c]

    def spread(ref, lead, at):
        return jnp.broadcast_to(ref[lead + (pl.ds(at, 1), slice(None))], (8, width))

    def section(s, number, low, count, positive, source, store):
        weight = SECTION_WEIGHTS[number]
        held = {}

        def q(offset):
            if offset not in held:
                held[offset] = source[low + offset]
            return held[offset]

        def along_x(face):
            flux = spread(flux_x_ref, (s,), low + face)
            if positive:
                five = (q(face - 3), q(face - 2), q(face - 1), q(face), q(face + 1))
            else:
                five = (q(face + 2), q(face + 1), q(face), q(face - 1), q(face - 2))
            a, b, c, d, e = five
            return flux * (((a - 6.5 * b) + (23.5 * c + 13.5 * d)) - 1.5 * e)

        before = along_x(0)
        for k in range(count):
            after = along_x(k + 1)
            here_q = q(k)
            terms = []
            for index in range(6):
                moved = here_q if index == 3 else shift(here_q, 3 - index)
                terms.append(spread(band_ref, (s, index), low + k) * moved)
            along_y = ((terms[0] + terms[1]) + (terms[2] + terms[3])) + (terms[4] + terms[5])
            div = (after - before) + (shift(along_y, -1) - along_y)
            if number == 0:
                start = here_q * spread(mass_row_ref, (s,), low + k)
                start_ref[low + k] = start
            else:
                start = start_ref[low + k]
            if weight != 1.0:
                start = start * (1.0 / weight)
            store(low + k, k, (start - div) * spread(inverse_ref, (s, number), low + k))
            before = after
            held.pop(k - 3, None)

    def level_body(level, carry):
        coefficients(level)
        for r in range(6, 24):
            at = pl.ds(level * cells + r, tracers, stride=levels * cells)
            q_a[r] = turned(low_ref[at, :], low_order)
        for r in range(cells):
            at = pl.ds(level * cells + r, tracers, stride=levels * cells)
            q_a[cells + r] = own_ref[at, :]
        for r in range(18):
            at = pl.ds(level * cells + r, tracers, stride=levels * cells)
            q_a[2 * cells + r] = turned(high_ref[at, :], high_order)

        reach = [jnp.where(sign_ref[s, level] > 0.0, 3, 2).astype(jnp.int32) for s in range(steps)]
        total = steps * 3
        lows = [None] * total
        lows[total - 1] = jnp.int32(cells)
        for n in range(total - 2, -1, -1):
            lows[n] = lows[n + 1] - reach[(n + 1) // 3]

        def out_store(at, k, value):
            out_ref[pl.ds(level * cells + k, tracers, stride=levels * cells), :] = value

        def into(ref):
            def store(at, k, value):
                ref[at] = value

            return store

        for s in range(steps):
            for positive in (True, False):

                @pl.when((sign_ref[s, level] > 0.0) == positive)
                def _():
                    last = out_store if s == steps - 1 else into(q_a)
                    plan = ((q_a, into(q_b)), (q_b, into(q_c)), (q_c, last))
                    for number, (source, store) in enumerate(plan):
                        n = s * 3 + number
                        section(s, number, lows[n], cells + 5 * (total - 1 - n), positive, source, store)

        return carry

    lax.fori_loop(0, levels, level_body, 0)


def local(tracers, wind_x, wind_y, surface_p, coef_a, coef_b, edge_flip):
    count, levels, cells, width = tracers.shape
    steps, block = wind_x.shape[0], wind_x.shape[3]
    groups, tiles = lax.axis_size("grp"), lax.axis_size("tile")
    used = (2 * levels + 1) * steps * block
    stride = -(-used // 8) * 8

    signs = wind_x[:, :, 0, 0, 0]
    packed = jnp.concatenate(
        [wind_x.reshape(-1, width), wind_y.reshape(-1, width), surface_p.reshape(-1, width)], axis=0
    )
    packed = jnp.pad(packed, ((0, stride - used), (0, 0)))
    low = lax.ppermute(tracers, "tile", ring(tiles, 1))
    high = lax.ppermute(tracers, "tile", ring(tiles, -1))
    met = lax.all_to_all(jnp.broadcast_to(packed[None], (groups, stride, width)), "grp", 0, 0, tiled=True)
    met_low = lax.ppermute(met, "tile", ring(tiles, 1))
    met_high = lax.ppermute(met, "tile", ring(tiles, -1))

    flat = (count * levels * cells, width)
    met_flat = (groups * stride, width)
    dims = (steps, levels, cells, block, groups, count, stride)
    rows = 3 * cells
    smem = pl.BlockSpec(memory_space=pltpu.SMEM)
    vmem = pl.BlockSpec(memory_space=pltpu.VMEM)
    out, mass = pl.pallas_call(
        functools.partial(advect_kernel, dims),
        out_shape=(
            jax.ShapeDtypeStruct(flat, jnp.float32),
            jax.ShapeDtypeStruct((levels * cells, width), jnp.float32),
        ),
        in_specs=[smem] * 4 + [vmem] * 6,
        out_specs=(vmem, vmem),
        scratch_shapes=[pltpu.VMEM((rows, count, width), jnp.float32)] * 4
        + [
            pltpu.VMEM((steps, rows, width), jnp.float32),
            pltpu.VMEM((steps, 6, rows, width), jnp.float32),
            pltpu.VMEM((steps, 3, rows, width), jnp.float32),
            pltpu.VMEM((steps, rows, width), jnp.float32),
        ],
        compiler_params=pltpu.CompilerParams(vmem_limit_bytes=VMEM_LIMIT),
        name="advect",
    )(
        signs,
        edge_flip,
        coef_a,
        coef_b,
        tracers.reshape(flat),
        low.reshape(flat),
        high.reshape(flat),
        met.reshape(met_flat),
        met_low.reshape(met_flat),
        met_high.reshape(met_flat),
    )
    return out.reshape(tracers.shape), mass.reshape(levels, cells, width)


def solution(mesh):
    return jax.shard_map(
        local,
        mesh=mesh,
        in_specs=(
            P("grp", None, "tile", None),
            P(None, None, "tile", "grp", None),
            P(None, None, "tile", "grp", None),
            P(None, "tile", "grp", None),
            P(),
            P(),
            P(),
        ),
        out_specs=(P("grp", None, "tile", None), P(None, "tile", None)),
        check_vma=False,
    )
```

profile of v0, /device:TPU:2, one launch (start us, length us, event | category | flops | bytes accessed | tf_op | source)
XLA Modules:
  0.0 168.7 jit_solution(18075647966319259429)
XLA Ops:
  0.6 0.7 reduce.3
  1.3 0.8 reduce.2
  2.2 0.0 copy-start.4
  2.2 0.7 copy-done.4
  2.9 0.0 copy-start
  2.9 0.1 reduce.1
  3.0 0.8 broadcast_in_dim.2
  3.9 6.0 %all-to-all-start = ((f32[8,120,128]{2,1,0:T(8,128)}), f32[8,120,128]{2,1,0:T(8,128)S(1)}, u32[]{:S(2)}, u32[]{:S(2)}) async-start(f32[8,120,128]{2,1,0:T(8,128)} %broadcast_in_dim.2), calls=%async_computation | async-start | bytes 983040 | tf_op jit(solution)/shard_map/all_to_all | solution.py:249
  9.9 0.0 copy-done
  9.9 6.0 %collective-permute-start.1 = (f32[8,9,24,128]{3,2,1,0:T(8,128)S(1)}, f32[8,9,24,128]{3,2,1,0:T(8,128)S(1)}, u32[]{:S(2)}, u32[]{:S(2)}) collective-permute-start(f32[8,9,24,128]{3,2,1,0:T(8,128)S(1)} %copy-done), channel_id=1, source_target_pairs={{0,31},{1,0},{2,1},{3,2},{4,3},{5,4},{6,5},{7,6},{8,7},{9,8},{10,9... | collective-permute-start | bytes 2654216 | tf_op jit(solution)/shard_map/ppermute | solution.py:248
  15.9 0.0 collective-permute-start
  15.9 4.8 %all-to-all-done = f32[8,120,128]{2,1,0:T(8,128)S(1)} async-done(((f32[8,120,128]{2,1,0:T(8,128)}), f32[8,120,128]{2,1,0:T(8,128)S(1)}, u32[]{:S(2)}, u32[]{:S(2)}) %all-to-all-start) | async-done | bytes 491552 | tf_op jit(solution)/shard_map/all_to_all | solution.py:249
  20.7 12.8 %collective-permute-start.3 = (f32[8,120,128]{2,1,0:T(8,128)S(1)}, f32[8,120,128]{2,1,0:T(8,128)S(1)}, u32[]{:S(2)}, u32[]{:S(2)}) collective-permute-start(f32[8,120,128]{2,1,0:T(8,128)S(1)} %all-to-all-done), channel_id=1, source_target_pairs={{0,31},{1,0},{2,1},{3,2},{4,3},{5,4},{6,5},{7,6},{8,7},{9,8},{10,9... | collective-permute-start | bytes 1474568 | tf_op jit(solution)/shard_map/ppermute | solution.py:251
  33.5 0.0 collective-permute-start.2
  33.5 0.2 slice_reduce_fusion.sign_ref
  33.6 0.0 collective-permute-done.1
  33.6 0.0 collective-permute-done
  33.6 6.2 %collective-permute-done.3 = f32[8,120,128]{2,1,0:T(8,128)S(1)} collective-permute-done((f32[8,120,128]{2,1,0:T(8,128)S(1)}, f32[8,120,128]{2,1,0:T(8,128)S(1)}, u32[]{:S(2)}, u32[]{:S(2)}) %collective-permute-start.3) | collective-permute-done | bytes 491552 | tf_op jit(solution)/shard_map/ppermute | solution.py:251
  39.8 4.0 %collective-permute-done.2 = f32[8,120,128]{2,1,0:T(8,128)S(1)} collective-permute-done((f32[8,120,128]{2,1,0:T(8,128)S(1)}, f32[8,120,128]{2,1,0:T(8,128)S(1)}, u32[]{:S(2)}, u32[]{:S(2)}) %collective-permute-start.2) | collective-permute-done | bytes 491552 | tf_op jit(solution)/shard_map/ppermute | solution.py:250
  43.8 0.0 copy-start.1
  43.8 0.0 copy-start.2
  43.8 0.0 copy-start.3
  43.8 0.6 copy-done.1
  44.5 0.0 copy-done.2
  44.5 0.0 copy-done.3
  44.5 124.1 %advect.1 = (f32[1728,128]{1,0:T(8,128)}, f32[216,128]{1,0:T(8,128)}) custom-call(f32[2,9]{1,0:T(2,128)S(1)} %slice_reduce_fusion.sign_ref, s32[32]{0:T(128)S(1)} %copy-done.1, f32[9]{0:T(128)S(1)} %copy-done.2, f32[9]{0:T(128)S(1)} %copy-done.3, f32[1728,128]{1,0:T(8,128)S(1)} %bitcast.9, f32[1728,128]{1,0:T(8,128)S(1)} %bitcast.11, ...), custom_call_target="tpu_custom_call" | custom-call | tf_op jit(solution)/shard_map/advect/pallas_call | solution.py:259
  (4 shorter events, 0.1 us)
Async XLA Ops:
  2.2 0.7 copy-start.4
  2.9 7.0 %copy-start = (f32[8,9,24,128]{3,2,1,0:T(8,128)S(1)}, f32[8,9,24,128]{3,2,1,0:T(8,128)}, u32[]{:S(2)}) copy-start(f32[8,9,24,128]{3,2,1,0:T(8,128)} %param.7) | copy-start | bytes 2654212
  3.9 16.9 %all-to-all-start = ((f32[8,120,128]{2,1,0:T(8,128)}), f32[8,120,128]{2,1,0:T(8,128)S(1)}, u32[]{:S(2)}, u32[]{:S(2)}) async-start(f32[8,120,128]{2,1,0:T(8,128)} %broadcast_in_dim.2), calls=%async_computation | async-start | bytes 983040 | tf_op jit(solution)/shard_map/all_to_all | solution.py:249
  9.9 23.7 %collective-permute-start.1 = (f32[8,9,24,128]{3,2,1,0:T(8,128)S(1)}, f32[8,9,24,128]{3,2,1,0:T(8,128)S(1)}, u32[]{:S(2)}, u32[]{:S(2)}) collective-permute-start(f32[8,9,24,128]{3,2,1,0:T(8,128)S(1)} %copy-done), channel_id=1, source_target_pairs={{0,31},{1,0},{2,1},{3,2},{4,3},{5,4},{6,5},{7,6},{8,7},{9,8},{10,9... | collective-permute-start | bytes 2654216 | tf_op jit(solution)/shard_map/ppermute | solution.py:248
  15.9 17.8 %collective-permute-start = (f32[8,9,24,128]{3,2,1,0:T(8,128)S(1)}, f32[8,9,24,128]{3,2,1,0:T(8,128)S(1)}, u32[]{:S(2)}, u32[]{:S(2)}) collective-permute-start(f32[8,9,24,128]{3,2,1,0:T(8,128)S(1)} %copy-done), channel_id=1, source_target_pairs={{0,1},{1,2},{2,3},{3,4},{4,5},{5,6},{6,7},{7,8},{8,9},{9,10},{10,1... | collective-permute-start | bytes 2654216 | tf_op jit(solution)/shard_map/ppermute | solution.py:247
  20.7 19.1 %collective-permute-start.3 = (f32[8,120,128]{2,1,0:T(8,128)S(1)}, f32[8,120,128]{2,1,0:T(8,128)S(1)}, u32[]{:S(2)}, u32[]{:S(2)}) collective-permute-start(f32[8,120,128]{2,1,0:T(8,128)S(1)} %all-to-all-done), channel_id=1, source_target_pairs={{0,31},{1,0},{2,1},{3,2},{4,3},{5,4},{6,5},{7,6},{8,7},{9,8},{10,9... | collective-permute-start | bytes 1474568 | tf_op jit(solution)/shard_map/ppermute | solution.py:251
  33.5 10.4 %collective-permute-start.2 = (f32[8,120,128]{2,1,0:T(8,128)S(1)}, f32[8,120,128]{2,1,0:T(8,128)S(1)}, u32[]{:S(2)}, u32[]{:S(2)}) collective-permute-start(f32[8,120,128]{2,1,0:T(8,128)S(1)} %all-to-all-done), channel_id=1, source_target_pairs={{0,1},{1,2},{2,3},{3,4},{4,5},{5,6},{6,7},{7,8},{8,9},{9,10},{10,1... | collective-permute-start | bytes 1474568 | tf_op jit(solution)/shard_map/ppermute | solution.py:250
  43.8 0.7 copy-start.1
  43.8 0.7 copy-start.2
  43.8 0.7 copy-start.3
where the time goes:
time: 169 us
  Pallas kernels  124 us (73%)
  starting transfers between devices  24.8 us (15%)
  waiting for transfers between devices  15 us (9%)
  local copies, waits for them, and re-layouts  2.42 us (1%)
    pallas_call x1, Pallas kernels, local(): pl.pallas_call(functools.partial(advect_kernel, dims), out_shape=(jax.Sha...  124 us
    ppermute x1, starting transfers between devices, local(): met_high = lax.ppermute(met, 'tile', ring(tiles, -1))  12.8 us
    ppermute x1, waiting for transfers between devices, local(): met_high = lax.ppermute(met, 'tile', ring(tiles, -1))  6.18 us
    all_to_all x1, starting transfers between devices, local(): lax.all_to_all(jnp.broadcast_to(packed[None], (groups, stride, width)), '...  6.03 us
    ppermute x1, starting transfers between devices, local(): high = lax.ppermute(tracers, 'tile', ring(tiles, -1))  5.96 us
    all_to_all x1, waiting for transfers between devices, local(): lax.all_to_all(jnp.broadcast_to(packed[None], (groups, stride, width)), '...  4.85 us
    ppermute x1, waiting for transfers between devices, local(): met_low = lax.ppermute(met, 'tile', ring(tiles, 1))  4.02 us
  transfers between devices with their start and end apart: 5, of which 3 were waited for; matrix products, arithmetic and copies ran while one was open for 0% of the time, Pallas kernels for 0%

commit v1 on v0

v1 whole, which is shorter than its diff:
```python
import functools

import jax
import jax.numpy as jnp
import ml_dtypes
import numpy as np
from jax import lax
from jax.experimental import pallas as pl
from jax.experimental.pallas import tpu as pltpu
from jax.sharding import PartitionSpec as P

SECTION_WEIGHTS = (1.0 / 3.0, 0.5, 1.0)
TOGETHER = 3
SLOTS = 32
VMEM_LIMIT = 48 * 1024 * 1024


def ring(count, step):
    return [(i, (i + step) % count) for i in range(count)]


def stencil_weights(width):
    out = np.zeros((2, 2 * width, 2 * width), np.float32)
    for side in range(2):
        for j in range(width):
            face = j + side
            for tap, value in enumerate((2.0, -13.0, 47.0, 27.0, -3.0)):
                up = min(max(face - 3 + tap, 0), width - 1)
                down = min(max(face + 2 - tap, 0), width - 1)
                for half in (0, width):
                    out[side, half + up, j] += value
                    out[side, half + down, width + j] += value
    return out.astype(ml_dtypes.bfloat16)


def advect_kernel(
    dims,
    sign_ref,
    flip_ref,
    gain_a_ref,
    gain_b_ref,
    own_ref,
    low_ref,
    high_ref,
    met_own_ref,
    met_low_ref,
    met_high_ref,
    weights_ref,
    out_ref,
    mass_ref,
    q_a,
    q_b,
    q_c,
    q_d,
    start_ref,
    coef_ref,
):
    steps, levels, cells, block, groups, tracers, stride = dims
    width = 128
    rows = 3 * cells
    tiles = lax.axis_size("tile")
    here = lax.axis_index("tile")
    low_flip = flip_ref[lax.rem(here + tiles - 1, tiles)]
    high_flip = flip_ref[here]

    lane = lax.broadcasted_iota(jnp.int32, (8, width), 1)
    row = lax.broadcasted_iota(jnp.int32, (8, width), 0)
    first_row = row == 0
    last_row = row == groups - 1

    def order_of(flip):
        return jnp.where(flip == 1, width - 1 - lane, lane)

    low_order = order_of(low_flip)
    high_order = order_of(high_flip)
    low_sign = jnp.where(low_flip == 1, -1.0, 1.0).astype(jnp.float32)
    high_sign = jnp.where(high_flip == 1, -1.0, 1.0).astype(jnp.float32)

    def turned(values, order):
        return jnp.take_along_axis(values, order, axis=1)

    def shift(values, by):
        return pltpu.roll(values, by % width, 1)

    def coefficients(level, slot):
        gain_a = gain_a_ref[level]
        gain_b = gain_b_ref[level]
        refs = (met_low_ref, met_own_ref, met_high_ref)
        orders = (low_order, None, high_order)
        signs = (low_sign, None, high_sign)
        mass = None
        for s in range(steps):
            flux_x = [[None] * block for _ in range(3)]
            flux_y = [[None] * block for _ in range(3)]
            start = [[None] * block for _ in range(3)]
            for t in range(3):
                for c in range(block):
                    at = s * levels * block + level * block + c
                    pressure = refs[t][pl.ds(2 * steps * levels * block + s * block + c, 8, stride=stride), :]
                    met = gain_a + gain_b * pressure
                    x = refs[t][pl.ds(at, 8, stride=stride), :] * met
                    y = refs[t][pl.ds(steps * levels * block + at, 8, stride=stride), :] * met
                    if orders[t] is not None:
                        x = turned(x, orders[t])
                        y = turned(y, orders[t]) * signs[t]
                        if s == 0:
                            met = turned(met, orders[t])
                    flux_x[t][c] = x
                    flux_y[t][c] = y
                    start[t][c] = met
            if s == 0:
                mass = start
            face_x = [[None] * block for _ in range(3)]
            for t in range(3):
                for c in range(block):
                    if c:
                        before = flux_x[t][c - 1]
                    else:
                        before = pltpu.roll(flux_x[t][block - 1], 1, 0)
                        if t:
                            before = jnp.where(first_row, pltpu.roll(flux_x[t - 1][block - 1], 1, 0), before)
                    face_x[t][c] = 0.5 * (before + flux_x[t][c])
            for t in range(3):
                for c in range(block):
                    if c < block - 1:
                        after = face_x[t][c + 1]
                    else:
                        after = pltpu.roll(face_x[t][0], groups - 1, 0)
                        if t < 2:
                            after = jnp.where(last_row, pltpu.roll(face_x[t + 1][0], groups - 1, 0), after)
                    face_y = jnp.where(lane == 0, 0.0, 0.5 * (shift(flux_y[t][c], 1) + flux_y[t][c]))
                    next_y = shift(face_y, -1)
                    div = (after - face_x[t][c]) + (next_y - face_y)
                    kinds = [jnp.abs(face_x[t][c]) * (1.0 / 30.0), face_y * (1.0 / 60.0), next_y * (1.0 / 60.0)]
                    for weight in SECTION_WEIGHTS:
                        kinds.append(weight / (mass[t][c] - weight * div))
                    kinds.append(mass[t][c])
                    for kind, value in enumerate(kinds):
                        coef_ref[slot, s, pl.ds((t * cells + c) * 8 + kind, 8, stride=8 * block), :] = value
                    mass[t][c] = mass[t][c] - div
        for c in range(block):
            mass_ref[pl.ds(level * cells + c, 8, stride=block), :] = mass[1][c]

    def run(*accs):
        for side in range(2):
            pltpu.matmul_push_rhs(weights_ref[side], 0, side)
        for side in range(2):
            pltpu.matmul_acc_lhs(accs[side], jnp.zeros((16, 256), jnp.bfloat16), load_staged_rhs=0)
            out_ref[0:16, :] = pltpu.matmul_pop(accs[side])[:, :width]

        def group_body(group, carry):
            flow = []
            for slot in range(TOGETHER):
                level = group * TOGETHER + slot
                coefficients(level, slot)
                ahead = [sign_ref[s, level] > 0.0 for s in range(steps)]
                way = [jnp.where(a, 1, -1).astype(jnp.int32) for a in ahead]
                same = way[0] == way[1]
                first = jnp.where(same, cells - 9, cells - 6)
                inlet = [first - 6, jnp.int32(cells - 6)]
                base = [jnp.where(a, p, rows - 1 - p) for a, p in zip(ahead, inlet)]
                for r in range(6, rows - 6):
                    ref, order = ((low_ref, low_order), (own_ref, None), (high_ref, high_order))[r // cells]
                    value = ref[pl.ds(level * cells + r % cells, tracers, stride=levels * cells), :]
                    if order is not None:
                        value = turned(value, order)
                    q_a[slot, (r - base[0]) * way[0] + 6] = value
                flow.append((level, ahead, way, same, base))

            plan = [
                (0, 0, q_a, 3, q_b),
                (0, 1, q_b, 0, q_c),
                (0, 2, q_c, 0, q_d),
                (1, 0, q_d, 0, q_b),
                (1, 1, q_b, 0, q_c),
                (1, 2, q_c, 0, None),
            ]
            items = [(n, slot) for n in range(6) for slot in range(TOGETHER)]
            counts = [cells + 5 * (5 - n) for n in range(6)]
            parts = [-(-c // 2) for c in counts]
            pushed, popped = [0], [0]

            def push(item, part):
                n, slot = item
                _, _, source, pad, _ = plan[n]
                at = 2 * part + 3 + pad
                both = jnp.concatenate([source[slot, at], source[slot, at + 1]], axis=0)
                high = both.astype(jnp.bfloat16)
                rest = (both - high.astype(jnp.float32)).astype(jnp.bfloat16)
                lhs = jnp.concatenate([high, rest], axis=1)
                place = pushed[0] % SLOTS
                pushed[0] += 1
                for side in range(2):
                    pltpu.matmul_acc_lhs(accs[2 * place + side], lhs)

            state = {}

            def finish(item, part):
                n, slot = item
                s, number, source, pad, target = plan[n]
                level, ahead, way, same, base = flow[slot]
                weight = SECTION_WEIGHTS[number]
                place = popped[0] % SLOTS
                popped[0] += 1
                pops = [pltpu.matmul_pop(accs[2 * place + side]) for side in range(2)]
                if part == 0:
                    state.clear()

                def spot(k):
                    return base[s] + way[s] * (k + 3 * number)

                def spread(at, kind):
                    return jnp.broadcast_to(coef_ref[slot, s, pl.ds(at * 8 + kind, 1), :], (8, width))

                def q(k):
                    if k not in state:
                        state[k] = source[slot, k + pad]
                    return state[k]

                def along_x(k):
                    at = spot(k) + jnp.where(ahead[s], 0, 1)
                    five = ((q(k) - 6.5 * q(k + 1)) + (23.5 * q(k + 2) + 13.5 * q(k + 3))) - 1.5 * q(k + 4)
                    return spread(at, 0) * five

                if part == 0:
                    state["before"] = along_x(0)
                for half in range(2):
                    k = 2 * part + half
                    if k >= counts[n]:
                        continue
                    at = spot(k)
                    after = along_x(k + 1)
                    sides = []
                    for side in range(2):
                        flux = spread(at, 1 + side)
                        rows_of = pops[side][8 * half : 8 * half + 8]
                        sides.append(flux * jnp.where(flux >= 0.0, rows_of[:, :width], rows_of[:, width:]))
                    div = (after - state["before"]) + (sides[1] - sides[0])
                    if number == 0:
                        start = q(k + 3) * spread(at, 6)
                        start_ref[slot, k] = start
                    else:
                        start = start_ref[slot, k + 3 * number]
                    if weight != 1.0:
                        start = start * (1.0 / weight)
                    value = (start - div) * spread(at, 3 + number)
                    if target is None:
                        i = jnp.where(ahead[1], k, cells - 1 - k)
                        out_ref[pl.ds(level * cells + i, tracers, stride=levels * cells), :] = value
                    elif target is q_d:
                        q_d[slot, jnp.where(same, k, counts[n] - 1 - k)] = value
                    else:
                        target[slot, k] = value
                    state["before"] = after
                    state.pop(k, None)

            for part in range(parts[0]):
                push(items[0], part)
            for index, item in enumerate(items):
                following = items[index + 1] if index + 1 < len(items) else None
                ahead_parts = parts[following[0]] if following else 0
                for part in range(max(parts[item[0]], ahead_parts)):
                    if part < parts[item[0]]:
                        finish(item, part)
                    if part < ahead_parts:
                        push(following, part)
            return carry

        lax.fori_loop(0, levels // TOGETHER, group_body, 0)

    acc = [pltpu.ACC(side)((16, 256), jnp.float32) for _ in range(SLOTS) for side in range(2)]
    pl.run_scoped(run, *acc)


def local(tracers, wind_x, wind_y, surface_p, coef_a, coef_b, edge_flip):
    count, levels, cells, width = tracers.shape
    steps, block = wind_x.shape[0], wind_x.shape[3]
    groups, tiles = lax.axis_size("grp"), lax.axis_size("tile")
    used = (2 * levels + 1) * steps * block
    stride = -(-used // 8) * 8

    signs = wind_x[:, :, 0, 0, 0]
    packed = jnp.concatenate(
        [wind_x.reshape(-1, width), wind_y.reshape(-1, width), surface_p.reshape(-1, width)], axis=0
    )
    packed = jnp.pad(packed, ((0, stride - used), (0, 0)))
    low = lax.ppermute(tracers, "tile", ring(tiles, 1))
    high = lax.ppermute(tracers, "tile", ring(tiles, -1))
    met = lax.all_to_all(jnp.broadcast_to(packed[None], (groups, stride, width)), "grp", 0, 0, tiled=True)
    met_low = lax.ppermute(met, "tile", ring(tiles, 1))
    met_high = lax.ppermute(met, "tile", ring(tiles, -1))

    flat = (count * levels * cells, width)
    met_flat = (groups * stride, width)
    dims = (steps, levels, cells, block, groups, count, stride)
    rows = 3 * cells
    smem = pl.BlockSpec(memory_space=pltpu.SMEM)
    vmem = pl.BlockSpec(memory_space=pltpu.VMEM)
    out, mass = pl.pallas_call(
        functools.partial(advect_kernel, dims),
        out_shape=(
            jax.ShapeDtypeStruct(flat, jnp.float32),
            jax.ShapeDtypeStruct((levels * cells, width), jnp.float32),
        ),
        in_specs=[smem] * 4 + [vmem] * 7,
        out_specs=(vmem, vmem),
        scratch_shapes=[
            pltpu.VMEM((TOGETHER, 64, count, width), jnp.float32),
            pltpu.VMEM((TOGETHER, 56, count, width), jnp.float32),
            pltpu.VMEM((TOGETHER, 56, count, width), jnp.float32),
            pltpu.VMEM((TOGETHER, 40, count, width), jnp.float32),
            pltpu.VMEM((TOGETHER, 56, count, width), jnp.float32),
            pltpu.VMEM((TOGETHER, steps, rows * 8, width), jnp.float32),
        ],
        compiler_params=pltpu.CompilerParams(vmem_limit_bytes=VMEM_LIMIT),
        name="advect",
    )(
        signs,
        edge_flip,
        coef_a,
        coef_b,
        tracers.reshape(flat),
        low.reshape(flat),
        high.reshape(flat),
        met.reshape(met_flat),
        met_low.reshape(met_flat),
        met_high.reshape(met_flat),
        jnp.asarray(stencil_weights(width)),
    )
    return out.reshape(tracers.shape), mass.reshape(levels, cells, width)


def solution(mesh):
    return jax.shard_map(
        local,
        mesh=mesh,
        in_specs=(
            P("grp", None, "tile", None),
            P(None, None, "tile", "grp", None),
            P(None, None, "tile", "grp", None),
            P(None, "tile", "grp", None),
            P(),
            P(),
            P(),
        ),
        out_specs=(P("grp", None, "tile", None), P(None, "tile", None)),
        check_vma=False,
    )
```

time: 169 us -> 58.6 us (0.35)
  Pallas kernels: 124 us -> 13.6 us
    pallas_call x1, Pallas kernels: 124 us -> 13.6 us  [local(): pl.pallas_call(functools.partial(advect_kernel, dims), out_shape=(jax.Sha...]
where the time goes in v1:
time: 58.6 us; the launch traced here: 58.2 us
  starting transfers between devices  24.9 us (42%)
  waiting for transfers between devices  15 us (26%)
  Pallas kernels  13.6 us (23%)
  local copies, waits for them, and re-layouts  2.41 us (4%)
  other arithmetic  1.62 us (3%)
  between operations  0.68 us (1%)
    pallas_call x1, Pallas kernels, local(): pl.pallas_call(functools.partial(advect_kernel, dims), out_shape=(jax.Sha...  13.6 us
    ppermute x1, starting transfers between devices, local(): met_high = lax.ppermute(met, 'tile', ring(tiles, -1))  12.8 us
    ppermute x1, waiting for transfers between devices, local(): met_high = lax.ppermute(met, 'tile', ring(tiles, -1))  6.18 us
    all_to_all x1, starting transfers between devices, local(): lax.all_to_all(jnp.broadcast_to(packed[None], (groups, stride, width)), '...  6.16 us
    ppermute x1, starting transfers between devices, local(): high = lax.ppermute(tracers, 'tile', ring(tiles, -1))  5.96 us
    all_to_all x1, waiting for transfers between devices, local(): lax.all_to_all(jnp.broadcast_to(packed[None], (groups, stride, width)), '...  4.85 us
    ppermute x1, waiting for transfers between devices, local(): met_low = lax.ppermute(met, 'tile', ring(tiles, 1))  4.02 us
    unnamed x3, other arithmetic  1.61 us
  transfers between devices with their start and end apart: 5, of which 3 were waited for; matrix products, arithmetic and copies ran while one was open for 0% of the time, Pallas kernels for 0%

profile of v1, /device:TPU:2, one launch (start us, length us, event | category | flops | bytes accessed | tf_op | source)
XLA Modules:
  0.0 58.2 jit_solution(4444527663645053499)
XLA Ops:
  0.6 0.7 %reduce.3 = f32[2,3,128]{2,1,0:T(4,128)S(1)} reduce(f32[2,1,3,128]{3,1,2,0:T(1,128)} %param.11, f32[]{:T(128)} %constant.12), dimensions={1}, to_apply=%param.11.reduce_sub_computation | reduce | bytes 6148 | tf_op args[3]
  1.3 0.8 %reduce.2 = f32[2,9,3,128]{3,2,1,0:T(4,128)S(1)} reduce(f32[2,9,1,3,128]{4,2,3,1,0:T(1,128)} %param.10, f32[]{:T(128)} %constant.12), dimensions={2}, to_apply=%param.10.reduce_sub_computation | reduce | bytes 55300 | tf_op args[2]
  2.2 0.0 copy-start.5
  2.2 0.7 %copy-done.5 = f32[2,9,1,3,128]{4,2,3,1,0:T(1,128)S(1)} copy-done((f32[2,9,1,3,128]{4,2,3,1,0:T(1,128)S(1)}, f32[2,9,1,3,128]{4,2,3,1,0:T(1,128)}, u32[]{:S(2)}) %copy-start.5) | copy-done | bytes 27672
  2.9 0.0 copy-start
  2.9 0.1 reduce.1
  3.0 0.8 %broadcast_in_dim.2 = f32[8,120,128]{2,1,0:T(8,128)} broadcast(f32[120,128]{1,0:T(8,128)S(1)} %select_maximum_fusion), dimensions={1,2} | broadcast | bytes 552960 | tf_op jit(solution)/shard_map/broadcast_in_dim | solution.py:289
  3.9 0.0 copy-start.1
  3.9 6.2 %all-to-all-start = ((f32[8,120,128]{2,1,0:T(8,128)}), f32[8,120,128]{2,1,0:T(8,128)S(1)}, u32[]{:S(2)}, u32[]{:S(2)}) async-start(f32[8,120,128]{2,1,0:T(8,128)} %broadcast_in_dim.2), calls=%async_computation | async-start | bytes 983040 | tf_op jit(solution)/shard_map/all_to_all | solution.py:289
  10.0 0.0 copy-done
  10.0 6.0 %collective-permute-start.1 = (f32[8,9,24,128]{3,2,1,0:T(8,128)S(1)}, f32[8,9,24,128]{3,2,1,0:T(8,128)S(1)}, u32[]{:S(2)}, u32[]{:S(2)}) collective-permute-start(f32[8,9,24,128]{3,2,1,0:T(8,128)S(1)} %copy-done), channel_id=1, source_target_pairs={{0,31},{1,0},{2,1},{3,2},{4,3},{5,4},{6,5},{7,6},{8,7},{9,8},{10,9... | collective-permute-start | bytes 2654216 | tf_op jit(solution)/shard_map/ppermute | solution.py:288
  16.0 0.0 collective-permute-start
  16.0 4.8 %all-to-all-done = f32[8,120,128]{2,1,0:T(8,128)S(1)} async-done(((f32[8,120,128]{2,1,0:T(8,128)}), f32[8,120,128]{2,1,0:T(8,128)S(1)}, u32[]{:S(2)}, u32[]{:S(2)}) %all-to-all-start) | async-done | bytes 491552 | tf_op jit(solution)/shard_map/all_to_all | solution.py:289
  20.8 12.8 %collective-permute-start.3 = (f32[8,120,128]{2,1,0:T(8,128)S(1)}, f32[8,120,128]{2,1,0:T(8,128)S(1)}, u32[]{:S(2)}, u32[]{:S(2)}) collective-permute-start(f32[8,120,128]{2,1,0:T(8,128)S(1)} %all-to-all-done), channel_id=1, source_target_pairs={{0,31},{1,0},{2,1},{3,2},{4,3},{5,4},{6,5},{7,6},{8,7},{9,8},{10,9... | collective-permute-start | bytes 1474568 | tf_op jit(solution)/shard_map/ppermute | solution.py:291
  33.6 0.0 collective-permute-start.2
  33.6 0.2 slice_reduce_fusion.sign_ref
  33.8 0.0 collective-permute-done.1
  33.8 0.0 collective-permute-done
  33.8 6.2 %collective-permute-done.3 = f32[8,120,128]{2,1,0:T(8,128)S(1)} collective-permute-done((f32[8,120,128]{2,1,0:T(8,128)S(1)}, f32[8,120,128]{2,1,0:T(8,128)S(1)}, u32[]{:S(2)}, u32[]{:S(2)}) %collective-permute-start.3) | collective-permute-done | bytes 491552 | tf_op jit(solution)/shard_map/ppermute | solution.py:291
  39.9 4.0 %collective-permute-done.2 = f32[8,120,128]{2,1,0:T(8,128)S(1)} collective-permute-done((f32[8,120,128]{2,1,0:T(8,128)S(1)}, f32[8,120,128]{2,1,0:T(8,128)S(1)}, u32[]{:S(2)}, u32[]{:S(2)}) %collective-permute-start.2) | collective-permute-done | bytes 491552 | tf_op jit(solution)/shard_map/ppermute | solution.py:290
  44.0 0.0 copy-start.2
  44.0 0.0 copy-start.3
  44.0 0.0 copy-start.4
  44.0 0.0 copy-done.1
  44.0 0.6 %copy-done.2 = s32[32]{0:T(128)S(1)} copy-done((s32[32]{0:T(128)S(1)}, s32[32]{0:T(128)}, u32[]{:S(2)}) %copy-start.2) | copy-done | bytes 152
  44.6 0.0 copy-done.3
  44.6 0.0 copy-done.4
  44.7 13.6 %advect.1 = (f32[1728,128]{1,0:T(8,128)}, f32[216,128]{1,0:T(8,128)}) custom-call(f32[2,9]{1,0:T(2,128)S(1)} %slice_reduce_fusion.sign_ref, s32[32]{0:T(128)S(1)} %copy-done.2, f32[9]{0:T(128)S(1)} %copy-done.3, f32[9]{0:T(128)S(1)} %copy-done.4, f32[1728,128]{1,0:T(8,128)S(1)} %bitcast.9, f32[1728,128]{1,0:T(8,128)S(1)} %bitcast.11, ...), custom_call_target="tpu_custom_call" | custom-call | tf_op jit(solution)/shard_map/advect/pallas_call | solution.py:299
  (4 shorter events, 0.1 us)
Async XLA Ops:
  2.2 0.7 %copy-start.5 = (f32[2,9,1,3,128]{4,2,3,1,0:T(1,128)S(1)}, f32[2,9,1,3,128]{4,2,3,1,0:T(1,128)}, u32[]{:S(2)}) copy-start(f32[2,9,1,3,128]{4,2,3,1,0:T(1,128)} %param.9) | copy-start | bytes 82948
  2.9 7.1 %copy-start = (f32[8,9,24,128]{3,2,1,0:T(8,128)S(1)}, f32[8,9,24,128]{3,2,1,0:T(8,128)}, u32[]{:S(2)}) copy-start(f32[8,9,24,128]{3,2,1,0:T(8,128)} %param.8) | copy-start | bytes 2654212
  3.9 40.1 %copy-start.1 = (bf16[2,256,256]{2,1,0:T(8,128)(2,1)S(1)}, bf16[2,256,256]{2,1,0:T(8,128)(2,1)}, u32[]{:S(2)}) copy-start(bf16[2,256,256]{2,1,0:T(8,128)(2,1)} %constant.5.clone.weights_ref) | copy-start | bytes 786436
  3.9 17.0 %all-to-all-start = ((f32[8,120,128]{2,1,0:T(8,128)}), f32[8,120,128]{2,1,0:T(8,128)S(1)}, u32[]{:S(2)}, u32[]{:S(2)}) async-start(f32[8,120,128]{2,1,0:T(8,128)} %broadcast_in_dim.2), calls=%async_computation | async-start | bytes 983040 | tf_op jit(solution)/shard_map/all_to_all | solution.py:289
  10.0 23.7 %collective-permute-start.1 = (f32[8,9,24,128]{3,2,1,0:T(8,128)S(1)}, f32[8,9,24,128]{3,2,1,0:T(8,128)S(1)}, u32[]{:S(2)}, u32[]{:S(2)}) collective-permute-start(f32[8,9,24,128]{3,2,1,0:T(8,128)S(1)} %copy-done), channel_id=1, source_target_pairs={{0,31},{1,0},{2,1},{3,2},{4,3},{5,4},{6,5},{7,6},{8,7},{9,8},{10,9... | collective-permute-start | bytes 2654216 | tf_op jit(solution)/shard_map/ppermute | solution.py:288
  16.0 17.8 %collective-permute-start = (f32[8,9,24,128]{3,2,1,0:T(8,128)S(1)}, f32[8,9,24,128]{3,2,1,0:T(8,128)S(1)}, u32[]{:S(2)}, u32[]{:S(2)}) collective-permute-start(f32[8,9,24,128]{3,2,1,0:T(8,128)S(1)} %copy-done), channel_id=1, source_target_pairs={{0,1},{1,2},{2,3},{3,4},{4,5},{5,6},{6,7},{7,8},{8,9},{9,10},{10,1... | collective-permute-start | bytes 2654216 | tf_op jit(solution)/shard_map/ppermute | solution.py:287
  20.8 19.1 %collective-permute-start.3 = (f32[8,120,128]{2,1,0:T(8,128)S(1)}, f32[8,120,128]{2,1,0:T(8,128)S(1)}, u32[]{:S(2)}, u32[]{:S(2)}) collective-permute-start(f32[8,120,128]{2,1,0:T(8,128)S(1)} %all-to-all-done), channel_id=1, source_target_pairs={{0,31},{1,0},{2,1},{3,2},{4,3},{5,4},{6,5},{7,6},{8,7},{9,8},{10,9... | collective-permute-start | bytes 1474568 | tf_op jit(solution)/shard_map/ppermute | solution.py:291
  33.6 10.4 %collective-permute-start.2 = (f32[8,120,128]{2,1,0:T(8,128)S(1)}, f32[8,120,128]{2,1,0:T(8,128)S(1)}, u32[]{:S(2)}, u32[]{:S(2)}) collective-permute-start(f32[8,120,128]{2,1,0:T(8,128)S(1)} %all-to-all-done), channel_id=1, source_target_pairs={{0,1},{1,2},{2,3},{3,4},{4,5},{5,6},{6,7},{7,8},{8,9},{9,10},{10,1... | collective-permute-start | bytes 1474568 | tf_op jit(solution)/shard_map/ppermute | solution.py:290
  44.0 0.7 %copy-start.2 = (s32[32]{0:T(128)S(1)}, s32[32]{0:T(128)}, u32[]{:S(2)}) copy-start(s32[32]{0:T(128)} %flip_ref.1) | copy-start | bytes 388
  44.0 0.7 %copy-start.3 = (f32[9]{0:T(128)S(1)}, f32[9]{0:T(128)}, u32[]{:S(2)}) copy-start(f32[9]{0:T(128)} %gain_a_ref.1) | copy-start | bytes 112
  44.0 0.7 %copy-start.4 = (f32[9]{0:T(128)S(1)}, f32[9]{0:T(128)}, u32[]{:S(2)}) copy-start(f32[9]{0:T(128)} %gain_b_ref.1) | copy-start | bytes 112

commit v2 on v1

--- a/solution.py
+++ b/solution.py
@@ -96,10 +96,10 @@
             for t in range(3):
                 for c in range(block):
                     at = s * levels * block + level * block + c
-                    pressure = refs[t][pl.ds(2 * steps * levels * block + s * block + c, 8, stride=stride), :]
+                    pressure = refs[t][pl.ds(112 + s * block + c, 8, stride=stride), :]
                     met = gain_a + gain_b * pressure
                     x = refs[t][pl.ds(at, 8, stride=stride), :] * met
-                    y = refs[t][pl.ds(steps * levels * block + at, 8, stride=stride), :] * met
+                    y = refs[t][pl.ds(56 + at, 8, stride=stride), :] * met
                     if orders[t] is not None:
                         x = turned(x, orders[t])
                         y = turned(y, orders[t]) * signs[t]
@@ -160,10 +160,14 @@
                 inlet = [first - 6, jnp.int32(cells - 6)]
                 base = [jnp.where(a, p, rows - 1 - p) for a, p in zip(ahead, inlet)]
                 for r in range(6, rows - 6):
-                    ref, order = ((low_ref, low_order), (own_ref, None), (high_ref, high_order))[r // cells]
-                    value = ref[pl.ds(level * cells + r % cells, tracers, stride=levels * cells), :]
-                    if order is not None:
-                        value = turned(value, order)
+                    if r < cells:
+                        at = (level * 18 + r - 6) * tracers
+                        value = turned(low_ref[pl.ds(pl.multiple_of(at, 8), tracers), :], low_order)
+                    elif r < 2 * cells:
+                        value = own_ref[pl.ds(level * cells + r - cells, tracers, stride=levels * cells), :]
+                    else:
+                        at = (level * 18 + r - 2 * cells) * tracers
+                        value = turned(high_ref[pl.ds(pl.multiple_of(at, 8), tracers), :], high_order)
                     q_a[slot, (r - base[0]) * way[0] + 6] = value
                 flow.append((level, ahead, way, same, base))
 
@@ -272,30 +276,59 @@
     pl.run_scoped(run, *acc)
 
 
+def edge_kernel(levels, cells, tracers, field_ref, up_ref, down_ref):
+    def level_body(level, carry):
+        for r in range(18):
+            at = pl.ds(pl.multiple_of((level * 18 + r) * tracers, 8), tracers)
+            up_ref[at, :] = field_ref[pl.ds(level * cells + cells - 18 + r, tracers, stride=levels * cells), :]
+            down_ref[at, :] = field_ref[pl.ds(level * cells + r, tracers, stride=levels * cells), :]
+        return carry
+
+    lax.fori_loop(0, levels, level_body, 0)
+
+
+def met_kernel(groups, x_ref, y_ref, p_ref, out_ref):
+    for ref, first in ((x_ref, 0), (y_ref, 56), (p_ref, 112)):
+        count = ref.shape[0]
+        value = ref[...].reshape(count, ref.shape[2])
+        for g in range(groups):
+            out_ref[g, first : first + count, :] = value
+
+
 def local(tracers, wind_x, wind_y, surface_p, coef_a, coef_b, edge_flip):
     count, levels, cells, width = tracers.shape
     steps, block = wind_x.shape[0], wind_x.shape[3]
     groups, tiles = lax.axis_size("grp"), lax.axis_size("tile")
-    used = (2 * levels + 1) * steps * block
-    stride = -(-used // 8) * 8
+    stride = 120
+    smem = pl.BlockSpec(memory_space=pltpu.SMEM)
+    vmem = pl.BlockSpec(memory_space=pltpu.VMEM)
+    flat = (count * levels * cells, width)
+    edge = jax.ShapeDtypeStruct((levels * 18 * count, width), jnp.float32)
 
     signs = wind_x[:, :, 0, 0, 0]
-    packed = jnp.concatenate(
-        [wind_x.reshape(-1, width), wind_y.reshape(-1, width), surface_p.reshape(-1, width)], axis=0
-    )
-    packed = jnp.pad(packed, ((0, stride - used), (0, 0)))
-    low = lax.ppermute(tracers, "tile", ring(tiles, 1))
-    high = lax.ppermute(tracers, "tile", ring(tiles, -1))
-    met = lax.all_to_all(jnp.broadcast_to(packed[None], (groups, stride, width)), "grp", 0, 0, tiled=True)
+    up, down = pl.pallas_call(
+        functools.partial(edge_kernel, levels, cells, count),
+        out_shape=(edge, edge),
+        in_specs=[vmem],
+        out_specs=(vmem, vmem),
+        name="edges",
+    )(tracers.reshape(flat))
+    low = lax.ppermute(up, "tile", ring(tiles, 1))
+    high = lax.ppermute(down, "tile", ring(tiles, -1))
+    packed = pl.pallas_call(
+        functools.partial(met_kernel, groups),
+        out_shape=jax.ShapeDtypeStruct((groups, stride, width), jnp.float32),
+        in_specs=[vmem] * 3,
+        out_specs=vmem,
+        name="met",
+    )(wind_x.reshape(-1, 1, width), wind_y.reshape(-1, 1, width), surface_p.reshape(-1, 1, width))
+    met = lax.all_to_all(packed, "grp", 0, 0, tiled=True)
     met_low = lax.ppermute(met, "tile", ring(tiles, 1))
     met_high = lax.ppermute(met, "tile", ring(tiles, -1))
 
-    flat = (count * levels * cells, width)
     met_flat = (groups * stride, width)
     dims = (steps, levels, cells, block, groups, count, stride)
     rows = 3 * cells
-    smem = pl.BlockSpec(memory_space=pltpu.SMEM)
-    vmem = pl.BlockSpec(memory_space=pltpu.VMEM)
     out, mass = pl.pallas_call(
         functools.partial(advect_kernel, dims),
         out_shape=(
@@ -320,8 +353,8 @@
         coef_a,
         coef_b,
         tracers.reshape(flat),
-        low.reshape(flat),
-        high.reshape(flat),
+        low,
+        high,
         met.reshape(met_flat),
         met_low.reshape(met_flat),
         met_high.reshape(met_flat),

time: 58.6 us -> 48.4 us (0.83)
  starting transfers between devices: 24.9 us -> 15.8 us
  Pallas kernels: 13.6 us -> 17.6 us
  waiting for transfers between devices: 15 us -> 12 us
  other arithmetic: 1.62 us -> 0 us
  local copies, waits for them, and re-layouts: 2.41 us -> 1.53 us
    ppermute x1, starting transfers between devices: 12.8 us -> 3.78 us  [local(): met_high = lax.ppermute(met, 'tile', ring(tiles, -1))]
    pallas_call x0 -> x2, Pallas kernels: none -> 4.06 us  [the longest x1 2.46 us: local(): pl.pallas_call(functools.partial(edge_kernel, levels, cells, count), out_...]
    all_to_all x1, waiting for transfers between devices: 4.85 us -> 2.46 us  [local(): met = lax.all_to_all(packed, 'grp', 0, 0, tiled=True)]
    unnamed x3 -> x0, other arithmetic: 1.61 us -> none
    ppermute x2, waiting for transfers between devices: 0.01 us -> 1.47 us  [the longest x1 1.46 us: local(): low = lax.ppermute(up, 'tile', ring(tiles, 1))]
    ppermute x1, waiting for transfers between devices: 4.02 us -> 2.94 us  [local(): met_low = lax.ppermute(met, 'tile', ring(tiles, 1))]
    ppermute x1, waiting for transfers between devices: 6.18 us -> 5.1 us  [local(): met_high = lax.ppermute(met, 'tile', ring(tiles, -1))]
    broadcast_in_dim x1 -> x0, local copies, waits for them, and re-layouts: 0.81 us -> none  [local(): jnp.broadcast_to(packed[None], (groups, stride, width))]
  transfers between devices with their start and end apart: 5 -> 5, of which waited for: 3 -> 4; matrix products, arithmetic and copies ran while one was open for 0% -> 2% of each run, Pallas kernels for 0% -> 5%
where the time goes in v2:
time: 48.4 us; the launch traced here: 47.6 us
  Pallas kernels  17.6 us (36%)
  starting transfers between devices  15.8 us (33%)
  waiting for transfers between devices  12 us (25%)
  local copies, waits for them, and re-layouts  1.53 us (3%)
  between operations  0.66 us (1%)
    pallas_call x1, Pallas kernels, local(): pl.pallas_call(functools.partial(advect_kernel, dims), out_shape=(jax.Sha...  13.5 us
    all_to_all x1, starting transfers between devices, local(): met = lax.all_to_all(packed, 'grp', 0, 0, tiled=True)  6.16 us
    ppermute x1, starting transfers between devices, local(): high = lax.ppermute(down, 'tile', ring(tiles, -1))  5.89 us
    ppermute x1, waiting for transfers between devices, local(): met_high = lax.ppermute(met, 'tile', ring(tiles, -1))  5.1 us
    ppermute x1, starting transfers between devices, local(): met_high = lax.ppermute(met, 'tile', ring(tiles, -1))  3.78 us
    ppermute x1, waiting for transfers between devices, local(): met_low = lax.ppermute(met, 'tile', ring(tiles, 1))  2.94 us
    all_to_all x1, waiting for transfers between devices, local(): met = lax.all_to_all(packed, 'grp', 0, 0, tiled=True)  2.46 us
    pallas_call x1, Pallas kernels, local(): pl.pallas_call(functools.partial(edge_kernel, levels, cells, count), out_...  2.46 us
  transfers between devices with their start and end apart: 5, of which 4 were waited for; matrix products, arithmetic and copies ran while one was open for 2% of the time, Pallas kernels for 5%

profile of v2, /device:TPU:2, one launch (start us, length us, event | category | flops | bytes accessed | tf_op | source)
XLA Modules:
  0.0 47.6 jit_solution(5378193000262868858)
XLA Ops:
  0.6 1.6 %met.1 = f32[8,120,128]{2,1,0:T(8,128)} custom-call(f32[54,1,128]{2,1,0:T(1,128)} %bitcast.14, f32[54,1,128]{2,1,0:T(1,128)} %bitcast.15, f32[6,1,128]{2,1,0:T(1,128)} %bitcast.16), custom_call_target="tpu_custom_call" | custom-call | tf_op jit(solution)/shard_map/met/pallas_call | solution.py:318
  2.2 0.0 copy-start
  2.2 6.2 %all-to-all-start = ((f32[8,120,128]{2,1,0:T(8,128)}), f32[8,120,128]{2,1,0:T(8,128)S(1)}, u32[]{:S(2)}, u32[]{:S(2)}) async-start(f32[8,120,128]{2,1,0:T(8,128)} %met.1), calls=%async_computation | async-start | bytes 983040 | tf_op jit(solution)/shard_map/all_to_all | solution.py:325
  8.4 0.0 copy-start.1
  8.4 2.5 %edges.1 = (f32[1296,128]{1,0:T(8,128)}, f32[1296,128]{1,0:T(8,128)}) custom-call(f32[1728,128]{1,0:T(8,128)} %bitcast.9), custom_call_target="tpu_custom_call" | custom-call | tf_op jit(solution)/shard_map/edges/pallas_call | solution.py:309
  10.9 0.0 collective-permute-start
  10.9 5.9 %collective-permute-start.1 = (f32[1296,128]{1,0:T(8,128)}, f32[1296,128]{1,0:T(8,128)S(1)}, u32[]{:S(2)}, u32[]{:S(2)}) collective-permute-start(f32[1296,128]{1,0:T(8,128)} %get-tuple-element.7), channel_id=1, source_target_pairs={{0,31},{1,0},{2,1},{3,2},{4,3},{5,4},{6,5},{7,6},{8,7},{9,8},{10,9... | collective-permute-start | bytes 1990664 | tf_op jit(solution)/shard_map/ppermute | solution.py:317
  16.8 2.5 %all-to-all-done = f32[8,120,128]{2,1,0:T(8,128)S(1)} async-done(((f32[8,120,128]{2,1,0:T(8,128)}), f32[8,120,128]{2,1,0:T(8,128)S(1)}, u32[]{:S(2)}, u32[]{:S(2)}) %all-to-all-start) | async-done | bytes 491552 | tf_op jit(solution)/shard_map/all_to_all | solution.py:325
  19.2 3.8 %collective-permute-start.3 = (f32[8,120,128]{2,1,0:T(8,128)S(1)}, f32[8,120,128]{2,1,0:T(8,128)S(1)}, u32[]{:S(2)}, u32[]{:S(2)}) collective-permute-start(f32[8,120,128]{2,1,0:T(8,128)S(1)} %all-to-all-done), channel_id=1, source_target_pairs={{0,31},{1,0},{2,1},{3,2},{4,3},{5,4},{6,5},{7,6},{8,7},{9,8},{10,9... | collective-permute-start | bytes 1474568 | tf_op jit(solution)/shard_map/ppermute | solution.py:327
  23.0 0.0 collective-permute-start.2
  23.0 0.9 %slice_reduce_fusion.sign_ref = f32[2,9]{1,0:T(2,128)S(1)} fusion(f32[2,9,1,3,128]{4,2,3,1,0:T(1,128)} %param.9), kind=kLoop, calls=%fused_computation | loop fusion | bytes 144 | tf_op jit(solution)/shard_map/slice | solution.py:308
  23.9 1.5 %collective-permute-done.low_ref = f32[1296,128]{1,0:T(8,128)S(1)} collective-permute-done((f32[1296,128]{1,0:T(8,128)}, f32[1296,128]{1,0:T(8,128)S(1)}, u32[]{:S(2)}, u32[]{:S(2)}) %collective-permute-start) | collective-permute-done | bytes 663584 | tf_op jit(solution)/shard_map/ppermute | solution.py:316
  25.3 0.0 collective-permute-done.1.high_ref
  25.3 5.1 %collective-permute-done.3 = f32[8,120,128]{2,1,0:T(8,128)S(1)} collective-permute-done((f32[8,120,128]{2,1,0:T(8,128)S(1)}, f32[8,120,128]{2,1,0:T(8,128)S(1)}, u32[]{:S(2)}, u32[]{:S(2)}) %collective-permute-start.3) | collective-permute-done | bytes 491552 | tf_op jit(solution)/shard_map/ppermute | solution.py:327
  30.4 2.9 %collective-permute-done.2 = f32[8,120,128]{2,1,0:T(8,128)S(1)} collective-permute-done((f32[8,120,128]{2,1,0:T(8,128)S(1)}, f32[8,120,128]{2,1,0:T(8,128)S(1)}, u32[]{:S(2)}, u32[]{:S(2)}) %collective-permute-start.2) | collective-permute-done | bytes 491552 | tf_op jit(solution)/shard_map/ppermute | solution.py:326
  33.4 0.0 copy-start.2
  33.4 0.0 copy-start.3
  33.4 0.0 copy-start.4
  33.4 0.0 copy-done
  33.4 0.0 copy-done.1
  33.4 0.6 %copy-done.2 = s32[32]{0:T(128)S(1)} copy-done((s32[32]{0:T(128)S(1)}, s32[32]{0:T(128)}, u32[]{:S(2)}) %copy-start.2) | copy-done | bytes 152
  34.0 0.0 copy-done.3
  34.0 0.0 copy-done.4
  34.1 13.5 %advect.1 = (f32[1728,128]{1,0:T(8,128)}, f32[216,128]{1,0:T(8,128)}) custom-call(f32[2,9]{1,0:T(2,128)S(1)} %slice_reduce_fusion.sign_ref, s32[32]{0:T(128)S(1)} %copy-done.2, f32[9]{0:T(128)S(1)} %copy-done.3, f32[9]{0:T(128)S(1)} %copy-done.4, f32[1728,128]{1,0:T(8,128)S(1)} %bitcast.10, f32[1296,128]{1,0:T(8,128)S(1)} %collective-permute-done.low_ref, ...), custom_call_target="tpu_custom_call" | custom-call | tf_op jit(solution)/shard_map/advect/pallas_call | solution.py:332
Async XLA Ops:
  2.2 31.1 %copy-start = (f32[8,9,24,128]{3,2,1,0:T(8,128)S(1)}, f32[8,9,24,128]{3,2,1,0:T(8,128)}, u32[]{:S(2)}) copy-start(f32[8,9,24,128]{3,2,1,0:T(8,128)} %param.8) | copy-start | bytes 2654212
  2.2 17.0 %all-to-all-start = ((f32[8,120,128]{2,1,0:T(8,128)}), f32[8,120,128]{2,1,0:T(8,128)S(1)}, u32[]{:S(2)}, u32[]{:S(2)}) async-start(f32[8,120,128]{2,1,0:T(8,128)} %met.1), calls=%async_computation | async-start | bytes 983040 | tf_op jit(solution)/shard_map/all_to_all | solution.py:325
  8.4 25.0 %copy-start.1 = (bf16[2,256,256]{2,1,0:T(8,128)(2,1)S(1)}, bf16[2,256,256]{2,1,0:T(8,128)(2,1)}, u32[]{:S(2)}) copy-start(bf16[2,256,256]{2,1,0:T(8,128)(2,1)} %constant.2.clone.weights_ref) | copy-start | bytes 786436
  10.9 14.5 %collective-permute-start = (f32[1296,128]{1,0:T(8,128)}, f32[1296,128]{1,0:T(8,128)S(1)}, u32[]{:S(2)}, u32[]{:S(2)}) collective-permute-start(f32[1296,128]{1,0:T(8,128)} %get-tuple-element.6), channel_id=1, source_target_pairs={{0,1},{1,2},{2,3},{3,4},{4,5},{5,6},{6,7},{7,8},{8,9},{9,10},{10,1... | collective-permute-start | bytes 1990664 | tf_op jit(solution)/shard_map/ppermute | solution.py:316
  10.9 14.5 %collective-permute-start.1 = (f32[1296,128]{1,0:T(8,128)}, f32[1296,128]{1,0:T(8,128)S(1)}, u32[]{:S(2)}, u32[]{:S(2)}) collective-permute-start(f32[1296,128]{1,0:T(8,128)} %get-tuple-element.7), channel_id=1, source_target_pairs={{0,31},{1,0},{2,1},{3,2},{4,3},{5,4},{6,5},{7,6},{8,7},{9,8},{10,9... | collective-permute-start | bytes 1990664 | tf_op jit(solution)/shard_map/ppermute | solution.py:317
  19.2 11.2 %collective-permute-start.3 = (f32[8,120,128]{2,1,0:T(8,128)S(1)}, f32[8,120,128]{2,1,0:T(8,128)S(1)}, u32[]{:S(2)}, u32[]{:S(2)}) collective-permute-start(f32[8,120,128]{2,1,0:T(8,128)S(1)} %all-to-all-done), channel_id=1, source_target_pairs={{0,31},{1,0},{2,1},{3,2},{4,3},{5,4},{6,5},{7,6},{8,7},{9,8},{10,9... | collective-permute-start | bytes 1474568 | tf_op jit(solution)/shard_map/ppermute | solution.py:327
  23.0 10.4 %collective-permute-start.2 = (f32[8,120,128]{2,1,0:T(8,128)S(1)}, f32[8,120,128]{2,1,0:T(8,128)S(1)}, u32[]{:S(2)}, u32[]{:S(2)}) collective-permute-start(f32[8,120,128]{2,1,0:T(8,128)S(1)} %all-to-all-done), channel_id=1, source_target_pairs={{0,1},{1,2},{2,3},{3,4},{4,5},{5,6},{6,7},{7,8},{8,9},{9,10},{10,1... | collective-permute-start | bytes 1474568 | tf_op jit(solution)/shard_map/ppermute | solution.py:326
  33.4 0.7 %copy-start.2 = (s32[32]{0:T(128)S(1)}, s32[32]{0:T(128)}, u32[]{:S(2)}) copy-start(s32[32]{0:T(128)} %flip_ref.1) | copy-start | bytes 388
  33.4 0.7 %copy-start.3 = (f32[9]{0:T(128)S(1)}, f32[9]{0:T(128)}, u32[]{:S(2)}) copy-start(f32[9]{0:T(128)} %gain_a_ref.1) | copy-start | bytes 112
  33.4 0.7 %copy-start.4 = (f32[9]{0:T(128)S(1)}, f32[9]{0:T(128)}, u32[]{:S(2)}) copy-start(f32[9]{0:T(128)} %gain_b_ref.1) | copy-start | bytes 112

commit v3 on v2

--- a/solution.py
+++ b/solution.py
@@ -12,11 +12,13 @@
 SECTION_WEIGHTS = (1.0 / 3.0, 0.5, 1.0)
 TOGETHER = 3
 SLOTS = 32
-VMEM_LIMIT = 48 * 1024 * 1024
-
-
-def ring(count, step):
-    return [(i, (i + step) % count) for i in range(count)]
+VMEM_LIMIT = 24 * 1024 * 1024
+
+
+def pairs(count):
+    near = [(i, i ^ 1) for i in range(count)]
+    far = [(i, (i + (1 if i % 2 else -1)) % count) for i in range(count)]
+    return near, far
 
 
 def stencil_weights(width):
@@ -35,16 +37,13 @@
 
 def advect_kernel(
     dims,
-    sign_ref,
-    flip_ref,
-    gain_a_ref,
-    gain_b_ref,
+    table_ref,
     own_ref,
-    low_ref,
-    high_ref,
+    near_ref,
+    far_ref,
     met_own_ref,
-    met_low_ref,
-    met_high_ref,
+    met_near_ref,
+    met_far_ref,
     weights_ref,
     out_ref,
     mass_ref,
@@ -60,8 +59,11 @@
     rows = 3 * cells
     tiles = lax.axis_size("tile")
     here = lax.axis_index("tile")
-    low_flip = flip_ref[lax.rem(here + tiles - 1, tiles)]
-    high_flip = flip_ref[here]
+    gains = steps * levels
+    flips = gains + 2 * levels
+    low_flip = table_ref[flips + lax.rem(here + tiles - 1, tiles)]
+    high_flip = table_ref[flips + here]
+    odd = lax.rem(here, 2) == 1
 
     lane = lax.broadcasted_iota(jnp.int32, (8, width), 1)
     row = lax.broadcasted_iota(jnp.int32, (8, width), 0)
@@ -69,12 +71,17 @@
     last_row = row == groups - 1
 
     def order_of(flip):
-        return jnp.where(flip == 1, width - 1 - lane, lane)
+        return jnp.where(flip == 1.0, width - 1 - lane, lane)
 
     low_order = order_of(low_flip)
     high_order = order_of(high_flip)
-    low_sign = jnp.where(low_flip == 1, -1.0, 1.0).astype(jnp.float32)
-    high_sign = jnp.where(high_flip == 1, -1.0, 1.0).astype(jnp.float32)
+    low_sign = jnp.where(low_flip == 1.0, -1.0, 1.0).astype(jnp.float32)
+    high_sign = jnp.where(high_flip == 1.0, -1.0, 1.0).astype(jnp.float32)
+
+    odd_mask = jnp.where(odd, lane, lane - width) >= 0
+
+    def chosen(below, near, far):
+        return jnp.where(odd_mask, near, far) if below else jnp.where(odd_mask, far, near)
 
     def turned(values, order):
         return jnp.take_along_axis(values, order, axis=1)
@@ -83,9 +90,15 @@
         return pltpu.roll(values, by % width, 1)
 
     def coefficients(level, slot):
-        gain_a = gain_a_ref[level]
-        gain_b = gain_b_ref[level]
-        refs = (met_low_ref, met_own_ref, met_high_ref)
+        gain_a = table_ref[gains + level]
+        gain_b = table_ref[gains + levels + level]
+
+        def take(t, first):
+            at = pl.ds(first, 8, stride=stride)
+            if t == 1:
+                return met_own_ref[at, :]
+            return chosen(t == 0, met_near_ref[at, :], met_far_ref[at, :])
+
         orders = (low_order, None, high_order)
         signs = (low_sign, None, high_sign)
         mass = None
@@ -96,10 +109,10 @@
             for t in range(3):
                 for c in range(block):
                     at = s * levels * block + level * block + c
-                    pressure = refs[t][pl.ds(112 + s * block + c, 8, stride=stride), :]
+                    pressure = take(t, 112 + s * block + c)
                     met = gain_a + gain_b * pressure
-                    x = refs[t][pl.ds(at, 8, stride=stride), :] * met
-                    y = refs[t][pl.ds(56 + at, 8, stride=stride), :] * met
+                    x = take(t, at) * met
+                    y = take(t, 56 + at) * met
                     if orders[t] is not None:
                         x = turned(x, orders[t])
                         y = turned(y, orders[t]) * signs[t]
@@ -153,7 +166,7 @@
             for slot in range(TOGETHER):
                 level = group * TOGETHER + slot
                 coefficients(level, slot)
-                ahead = [sign_ref[s, level] > 0.0 for s in range(steps)]
+                ahead = [table_ref[s * levels + level] > 0.0 for s in range(steps)]
                 way = [jnp.where(a, 1, -1).astype(jnp.int32) for a in ahead]
                 same = way[0] == way[1]
                 first = jnp.where(same, cells - 9, cells - 6)
@@ -161,13 +174,13 @@
                 base = [jnp.where(a, p, rows - 1 - p) for a, p in zip(ahead, inlet)]
                 for r in range(6, rows - 6):
                     if r < cells:
-                        at = (level * 18 + r - 6) * tracers
-                        value = turned(low_ref[pl.ds(pl.multiple_of(at, 8), tracers), :], low_order)
+                        at = pl.ds(pl.multiple_of((level * 18 + r - 6) * tracers, 8), tracers)
+                        value = turned(chosen(True, near_ref[at, :], far_ref[at, :]), low_order)
                     elif r < 2 * cells:
                         value = own_ref[pl.ds(level * cells + r - cells, tracers, stride=levels * cells), :]
                     else:
-                        at = (level * 18 + r - 2 * cells) * tracers
-                        value = turned(high_ref[pl.ds(pl.multiple_of(at, 8), tracers), :], high_order)
+                        at = pl.ds(pl.multiple_of((level * 18 + r - 2 * cells) * tracers, 8), tracers)
+                        value = turned(chosen(False, near_ref[at, :], far_ref[at, :]), high_order)
                     q_a[slot, (r - base[0]) * way[0] + 6] = value
                 flow.append((level, ahead, way, same, base))
 
@@ -276,12 +289,16 @@
     pl.run_scoped(run, *acc)
 
 
-def edge_kernel(levels, cells, tracers, field_ref, up_ref, down_ref):
+def edge_kernel(levels, cells, tracers, field_ref, near_ref, far_ref):
+    even = lax.rem(lax.axis_index("tile"), 2) == 0
+    near_row = jnp.where(even, cells - 18, 0)
+    far_row = cells - 18 - near_row
+
     def level_body(level, carry):
         for r in range(18):
             at = pl.ds(pl.multiple_of((level * 18 + r) * tracers, 8), tracers)
-            up_ref[at, :] = field_ref[pl.ds(level * cells + cells - 18 + r, tracers, stride=levels * cells), :]
-            down_ref[at, :] = field_ref[pl.ds(level * cells + r, tracers, stride=levels * cells), :]
+            for ref, row in ((near_ref, near_row), (far_ref, far_row)):
+                ref[at, :] = field_ref[pl.ds(level * cells + row + r, tracers, stride=levels * cells), :]
         return carry
 
     lax.fori_loop(0, levels, level_body, 0)
@@ -305,16 +322,19 @@
     flat = (count * levels * cells, width)
     edge = jax.ShapeDtypeStruct((levels * 18 * count, width), jnp.float32)
 
-    signs = wind_x[:, :, 0, 0, 0]
-    up, down = pl.pallas_call(
+    near_pairs, far_pairs = pairs(tiles)
+    table = jnp.concatenate(
+        [wind_x[:, :, 0, 0, 0].reshape(-1), coef_a, coef_b, edge_flip.astype(jnp.float32)], axis=0
+    )
+    near, far = pl.pallas_call(
         functools.partial(edge_kernel, levels, cells, count),
         out_shape=(edge, edge),
         in_specs=[vmem],
         out_specs=(vmem, vmem),
         name="edges",
     )(tracers.reshape(flat))
-    low = lax.ppermute(up, "tile", ring(tiles, 1))
-    high = lax.ppermute(down, "tile", ring(tiles, -1))
+    near = lax.ppermute(near, "tile", near_pairs)
+    far = lax.ppermute(far, "tile", far_pairs)
     packed = pl.pallas_call(
         functools.partial(met_kernel, groups),
         out_shape=jax.ShapeDtypeStruct((groups, stride, width), jnp.float32),
@@ -323,8 +343,8 @@
         name="met",
     )(wind_x.reshape(-1, 1, width), wind_y.reshape(-1, 1, width), surface_p.reshape(-1, 1, width))
     met = lax.all_to_all(packed, "grp", 0, 0, tiled=True)
-    met_low = lax.ppermute(met, "tile", ring(tiles, 1))
-    met_high = lax.ppermute(met, "tile", ring(tiles, -1))
+    met_near = lax.ppermute(met, "tile", near_pairs)
+    met_far = lax.ppermute(met, "tile", far_pairs)
 
     met_flat = (groups * stride, width)
     dims = (steps, levels, cells, block, groups, count, stride)
@@ -335,7 +355,7 @@
             jax.ShapeDtypeStruct(flat, jnp.float32),
             jax.ShapeDtypeStruct((levels * cells, width), jnp.float32),
         ),
-        in_specs=[smem] * 4 + [vmem] * 7,
+        in_specs=[smem] + [vmem] * 7,
         out_specs=(vmem, vmem),
         scratch_shapes=[
             pltpu.VMEM((TOGETHER, 64, count, width), jnp.float32),
@@ -348,16 +368,13 @@
         compiler_params=pltpu.CompilerParams(vmem_limit_bytes=VMEM_LIMIT),
         name="advect",
     )(
-        signs,
-        edge_flip,
-        coef_a,
-        coef_b,
+        table,
         tracers.reshape(flat),
-        low,
-        high,
+        near,
+        far,
         met.reshape(met_flat),
-        met_low.reshape(met_flat),
-        met_high.reshape(met_flat),
+        met_near.reshape(met_flat),
+        met_far.reshape(met_flat),
         jnp.asarray(stencil_weights(width)),
     )
     return out.reshape(tracers.shape), mass.reshape(levels, cells, width)

time: 48.4 us -> 47.4 us (0.979)
  the two profiles are of different devices: /device:TPU:2 before, /device:TPU:4 now
where the time goes in v3:
time: 47.4 us; the launch traced here: 47 us
  Pallas kernels  18.4 us (39%)
  starting transfers between devices  17.5 us (37%)
  waiting for transfers between devices  8.84 us (19%)
  local copies, waits for them, and re-layouts  1.53 us (3%)
  between operations  0.66 us (1%)
    pallas_call x1, Pallas kernels, local(): pl.pallas_call(functools.partial(advect_kernel, dims), out_shape=(jax.Sha...  14.2 us
    all_to_all x1, starting transfers between devices, local(): met = lax.all_to_all(packed, 'grp', 0, 0, tiled=True)  7.57 us
    ppermute x1, starting transfers between devices, local(): far = lax.ppermute(far, 'tile', far_pairs)  6.6 us
    ppermute x1, waiting for transfers between devices, local(): met_far = lax.ppermute(met, 'tile', far_pairs)  5.27 us
    ppermute x1, waiting for transfers between devices, local(): far = lax.ppermute(far, 'tile', far_pairs)  3.57 us
    ppermute x1, starting transfers between devices, local(): met_far = lax.ppermute(met, 'tile', far_pairs)  3.37 us
    pallas_call x1, Pallas kernels, local(): pl.pallas_call(functools.partial(edge_kernel, levels, cells, count), out_...  2.55 us
    pallas_call x1, Pallas kernels, local(): pl.pallas_call(functools.partial(met_kernel, groups), out_shape=jax.Shape...  1.6 us
  transfers between devices with their start and end apart: 5, of which 2 were waited for; matrix products, arithmetic and copies ran while one was open for 2% of the time, Pallas kernels for 5%

profile of v3, /device:TPU:4, one launch (start us, length us, event | category | flops | bytes accessed | tf_op | source)
XLA Modules:
  0.0 47.0 jit_solution(4043164758802047418)
XLA Ops:
  0.6 1.6 %met.1 = f32[8,120,128]{2,1,0:T(8,128)} custom-call(f32[54,1,128]{2,1,0:T(1,128)} %bitcast.13, f32[54,1,128]{2,1,0:T(1,128)} %bitcast.14, f32[6,1,128]{2,1,0:T(1,128)} %bitcast.15), custom_call_target="tpu_custom_call" | custom-call | tf_op jit(solution)/shard_map/met/pallas_call | solution.py:338
  2.2 0.0 copy-start
  2.2 7.6 %all-to-all-start = ((f32[8,120,128]{2,1,0:T(8,128)}), f32[8,120,128]{2,1,0:T(8,128)S(1)}, u32[]{:S(2)}, u32[]{:S(2)}) async-start(f32[8,120,128]{2,1,0:T(8,128)} %met.1), calls=%async_computation | async-start | bytes 983040 | tf_op jit(solution)/shard_map/all_to_all | solution.py:345
  9.8 0.0 copy-start.1
  9.8 2.6 %edges.1 = (f32[1296,128]{1,0:T(8,128)}, f32[1296,128]{1,0:T(8,128)}) custom-call(f32[1728,128]{1,0:T(8,128)} %bitcast.9), custom_call_target="tpu_custom_call" | custom-call | tf_op jit(solution)/shard_map/edges/pallas_call | solution.py:329
  12.4 0.0 copy-start.4
  12.4 0.0 collective-permute-start
  12.4 6.6 %collective-permute-start.1 = (f32[1296,128]{1,0:T(8,128)}, f32[1296,128]{1,0:T(8,128)S(1)}, u32[]{:S(2)}, u32[]{:S(2)}) collective-permute-start(f32[1296,128]{1,0:T(8,128)} %get-tuple-element.7), channel_id=1, source_target_pairs={{0,31},{1,2},{2,1},{3,4},{4,3},{5,6},{6,5},{7,8},{8,7},{9,10},{10,... | collective-permute-start | bytes 1990664 | tf_op jit(solution)/shard_map/ppermute | solution.py:337
  19.0 0.0 all-to-all-done
  19.0 3.4 %collective-permute-start.3 = (f32[8,120,128]{2,1,0:T(8,128)S(1)}, f32[8,120,128]{2,1,0:T(8,128)S(1)}, u32[]{:S(2)}, u32[]{:S(2)}) collective-permute-start(f32[8,120,128]{2,1,0:T(8,128)S(1)} %all-to-all-done), channel_id=1, source_target_pairs={{0,31},{1,2},{2,1},{3,4},{4,3},{5,6},{6,5},{7,8},{8,7},{9,10},{10,... | collective-permute-start | bytes 1474568 | tf_op jit(solution)/shard_map/ppermute | solution.py:347
  22.3 0.0 collective-permute-start.2
  22.3 0.0 copy-done.4
  22.4 0.9 %slice_reduce_fusion = f32[2,9]{1,0:T(2,128)S(1)} fusion(f32[2,9,1,3,128]{4,2,3,1,0:T(1,128)} %param.9), kind=kLoop, calls=%fused_computation | loop fusion | bytes 144 | tf_op jit(solution)/shard_map/slice | solution.py:327
  23.2 0.0 copy-start.2
  23.2 0.0 copy-start.3
  23.2 0.1 reshape_squeeze.3
  23.3 0.6 %copy-done.2 = f32[9]{0:T(128)S(1)} copy-done((f32[9]{0:T(128)S(1)}, f32[9]{0:T(128)}, u32[]{:S(2)}) %copy-start.2) | copy-done | bytes 60
  23.9 0.0 copy-done.3
  23.9 0.1 pad_maximum_fusion.table_ref
  24.0 0.0 collective-permute-done.near_ref
  24.0 3.6 %collective-permute-done.1.far_ref = f32[1296,128]{1,0:T(8,128)S(1)} collective-permute-done((f32[1296,128]{1,0:T(8,128)}, f32[1296,128]{1,0:T(8,128)S(1)}, u32[]{:S(2)}, u32[]{:S(2)}) %collective-permute-start.1) | collective-permute-done | bytes 663584 | tf_op jit(solution)/shard_map/ppermute | solution.py:337
  27.5 5.3 %collective-permute-done.3 = f32[8,120,128]{2,1,0:T(8,128)S(1)} collective-permute-done((f32[8,120,128]{2,1,0:T(8,128)S(1)}, f32[8,120,128]{2,1,0:T(8,128)S(1)}, u32[]{:S(2)}, u32[]{:S(2)}) %collective-permute-start.3) | collective-permute-done | bytes 491552 | tf_op jit(solution)/shard_map/ppermute | solution.py:347
  32.8 0.0 collective-permute-done.2
  32.8 0.0 copy-done
  32.8 0.0 copy-done.1
  32.8 14.2 %advect.1 = (f32[1728,128]{1,0:T(8,128)}, f32[216,128]{1,0:T(8,128)}) custom-call(f32[68]{0:T(128)S(1)} %pad_maximum_fusion.table_ref, f32[1728,128]{1,0:T(8,128)S(1)} %bitcast.10, f32[1296,128]{1,0:T(8,128)S(1)} %collective-permute-done.near_ref, f32[1296,128]{1,0:T(8,128)S(1)} %collective-permute-done.1.far_ref, f32[960,128]{1,0:T(8,128)S(1)} %bitcast.11, ...), custom_call_target="tpu_custom_call" | custom-call | tf_op jit(solution)/shard_map/advect/pallas_call | solution.py:352
  (1 shorter events, 0.0 us)
Async XLA Ops:
  2.2 30.6 %copy-start = (f32[8,9,24,128]{3,2,1,0:T(8,128)S(1)}, f32[8,9,24,128]{3,2,1,0:T(8,128)}, u32[]{:S(2)}) copy-start(f32[8,9,24,128]{3,2,1,0:T(8,128)} %param.8) | copy-start | bytes 2654212
  2.2 16.7 %all-to-all-start = ((f32[8,120,128]{2,1,0:T(8,128)}), f32[8,120,128]{2,1,0:T(8,128)S(1)}, u32[]{:S(2)}, u32[]{:S(2)}) async-start(f32[8,120,128]{2,1,0:T(8,128)} %met.1), calls=%async_computation | async-start | bytes 983040 | tf_op jit(solution)/shard_map/all_to_all | solution.py:345
  9.8 23.0 %copy-start.1 = (bf16[2,256,256]{2,1,0:T(8,128)(2,1)S(1)}, bf16[2,256,256]{2,1,0:T(8,128)(2,1)}, u32[]{:S(2)}) copy-start(bf16[2,256,256]{2,1,0:T(8,128)(2,1)} %constant.2.clone.weights_ref) | copy-start | bytes 786436
  12.4 10.0 %copy-start.4 = (s32[32]{0:T(128)S(1)}, s32[32]{0:T(128)}, u32[]{:S(2)}) copy-start(s32[32]{0:T(128)} %param.14) | copy-start | bytes 388
  12.4 11.6 %collective-permute-start = (f32[1296,128]{1,0:T(8,128)}, f32[1296,128]{1,0:T(8,128)S(1)}, u32[]{:S(2)}, u32[]{:S(2)}) collective-permute-start(f32[1296,128]{1,0:T(8,128)} %get-tuple-element.6), channel_id=1, source_target_pairs={{0,1},{1,0},{2,3},{3,2},{4,5},{5,4},{6,7},{7,6},{8,9},{9,8},{10,11... | collective-permute-start | bytes 1990664 | tf_op jit(solution)/shard_map/ppermute | solution.py:336
  12.4 15.2 %collective-permute-start.1 = (f32[1296,128]{1,0:T(8,128)}, f32[1296,128]{1,0:T(8,128)S(1)}, u32[]{:S(2)}, u32[]{:S(2)}) collective-permute-start(f32[1296,128]{1,0:T(8,128)} %get-tuple-element.7), channel_id=1, source_target_pairs={{0,31},{1,2},{2,1},{3,4},{4,3},{5,6},{6,5},{7,8},{8,7},{9,10},{10,... | collective-permute-start | bytes 1990664 | tf_op jit(solution)/shard_map/ppermute | solution.py:337
  19.0 13.8 %collective-permute-start.3 = (f32[8,120,128]{2,1,0:T(8,128)S(1)}, f32[8,120,128]{2,1,0:T(8,128)S(1)}, u32[]{:S(2)}, u32[]{:S(2)}) collective-permute-start(f32[8,120,128]{2,1,0:T(8,128)S(1)} %all-to-all-done), channel_id=1, source_target_pairs={{0,31},{1,2},{2,1},{3,4},{4,3},{5,6},{6,5},{7,8},{8,7},{9,10},{10,... | collective-permute-start | bytes 1474568 | tf_op jit(solution)/shard_map/ppermute | solution.py:347
  22.3 10.5 %collective-permute-start.2 = (f32[8,120,128]{2,1,0:T(8,128)S(1)}, f32[8,120,128]{2,1,0:T(8,128)}, u32[]{:S(2)}, u32[]{:S(2)}) collective-permute-start(f32[8,120,128]{2,1,0:T(8,128)S(1)} %all-to-all-done), channel_id=1, source_target_pairs={{0,1},{1,0},{2,3},{3,2},{4,5},{5,4},{6,7},{7,6},{8,9},{9,8},{10,11... | collective-permute-start | bytes 1474568 | tf_op jit(solution)/shard_map/ppermute | solution.py:346
  23.2 0.7 %copy-start.2 = (f32[9]{0:T(128)S(1)}, f32[9]{0:T(128)}, u32[]{:S(2)}) copy-start(f32[9]{0:T(128)} %param.13) | copy-start | bytes 112
  23.2 0.7 %copy-start.3 = (f32[9]{0:T(128)S(1)}, f32[9]{0:T(128)}, u32[]{:S(2)}) copy-start(f32[9]{0:T(128)} %param.12) | copy-start | bytes 112

commit v4 on v3

--- a/solution.py
+++ b/solution.py
@@ -11,6 +11,8 @@
 
 SECTION_WEIGHTS = (1.0 / 3.0, 0.5, 1.0)
 TOGETHER = 3
+ROWS = 64
+KINDS = 7
 SLOTS = 32
 VMEM_LIMIT = 24 * 1024 * 1024
 
@@ -44,7 +46,7 @@
     met_own_ref,
     met_near_ref,
     met_far_ref,
-    weights_ref,
+    weights_hbm,
     out_ref,
     mass_ref,
     q_a,
@@ -53,6 +55,9 @@
     q_d,
     start_ref,
     coef_ref,
+    met_side_ref,
+    weights_ref,
+    weights_sem,
 ):
     steps, levels, cells, block, groups, tracers, stride = dims
     width = 128
@@ -73,8 +78,16 @@
     def order_of(flip):
         return jnp.where(flip == 1.0, width - 1 - lane, lane)
 
-    low_order = order_of(low_flip)
-    high_order = order_of(high_flip)
+    def neighbour_orders(flip):
+        flipped = flip == 1.0
+        order = order_of(flip)
+        before = jnp.where(flipped, jnp.minimum(order + 1, width - 1), jnp.maximum(order - 1, 0))
+        after = jnp.where(flipped, jnp.maximum(order - 1, 0), jnp.minimum(order + 1, width - 1))
+        return order, before, after
+
+    low_orders = neighbour_orders(low_flip)
+    high_orders = neighbour_orders(high_flip)
+    low_order, high_order = low_orders[0], high_orders[0]
     low_sign = jnp.where(low_flip == 1.0, -1.0, 1.0).astype(jnp.float32)
     high_sign = jnp.where(high_flip == 1.0, -1.0, 1.0).astype(jnp.float32)
 
@@ -93,33 +106,39 @@
         gain_a = table_ref[gains + level]
         gain_b = table_ref[gains + levels + level]
 
-        def take(t, first):
-            at = pl.ds(first, 8, stride=stride)
+        def take(t, s, first):
             if t == 1:
-                return met_own_ref[at, :]
-            return chosen(t == 0, met_near_ref[at, :], met_far_ref[at, :])
-
-        orders = (low_order, None, high_order)
+                return met_own_ref[pl.ds(s * ROWS + first, 8, stride=stride), :]
+            return met_side_ref[t // 2, pl.ds((0 if (t == 0) == (s == 0) else 3) * ROWS + first, 8, stride=ROWS), :]
+
+        orders = (low_orders, None, high_orders)
         signs = (low_sign, None, high_sign)
         mass = None
         for s in range(steps):
             flux_x = [[None] * block for _ in range(3)]
-            flux_y = [[None] * block for _ in range(3)]
+            faces_y = [[None] * block for _ in range(3)]
             start = [[None] * block for _ in range(3)]
             for t in range(3):
                 for c in range(block):
-                    at = s * levels * block + level * block + c
-                    pressure = take(t, 112 + s * block + c)
+                    at = level * block + c
+                    pressure = take(t, s, 2 * levels * block + c)
                     met = gain_a + gain_b * pressure
-                    x = take(t, at) * met
-                    y = take(t, 56 + at) * met
+                    x = take(t, s, at) * met
+                    y = take(t, s, levels * block + at) * met
                     if orders[t] is not None:
-                        x = turned(x, orders[t])
-                        y = turned(y, orders[t]) * signs[t]
+                        order, order_before, order_after = orders[t]
+                        x = turned(x, order)
+                        y = y * signs[t]
+                        y_before, y_after, y = turned(y, order_before), turned(y, order_after), turned(y, order)
                         if s == 0:
-                            met = turned(met, orders[t])
+                            met = turned(met, order)
+                    else:
+                        y_before, y_after = shift(y, 1), shift(y, -1)
                     flux_x[t][c] = x
-                    flux_y[t][c] = y
+                    faces_y[t][c] = (
+                        jnp.where(lane == 0, 0.0, 0.5 * (y_before + y)),
+                        jnp.where(lane == width - 1, 0.0, 0.5 * (y + y_after)),
+                    )
                     start[t][c] = met
             if s == 0:
                 mass = start
@@ -141,20 +160,31 @@
                         after = pltpu.roll(face_x[t][0], groups - 1, 0)
                         if t < 2:
                             after = jnp.where(last_row, pltpu.roll(face_x[t + 1][0], groups - 1, 0), after)
-                    face_y = jnp.where(lane == 0, 0.0, 0.5 * (shift(flux_y[t][c], 1) + flux_y[t][c]))
-                    next_y = shift(face_y, -1)
+                    face_y, next_y = faces_y[t][c]
                     div = (after - face_x[t][c]) + (next_y - face_y)
                     kinds = [jnp.abs(face_x[t][c]) * (1.0 / 30.0), face_y * (1.0 / 60.0), next_y * (1.0 / 60.0)]
                     for weight in SECTION_WEIGHTS:
                         kinds.append(weight / (mass[t][c] - weight * div))
                     kinds.append(mass[t][c])
                     for kind, value in enumerate(kinds):
-                        coef_ref[slot, s, pl.ds((t * cells + c) * 8 + kind, 8, stride=8 * block), :] = value
+                        coef_ref[slot, s, pl.ds((t * cells + c) * KINDS + kind, 8, stride=KINDS * block), :] = value
                     mass[t][c] = mass[t][c] - div
         for c in range(block):
             mass_ref[pl.ds(level * cells + c, 8, stride=block), :] = mass[1][c]
 
     def run(*accs):
+        fetch = pltpu.make_async_copy(weights_hbm, weights_ref, weights_sem)
+        fetch.start()
+        met_side_ref[0, 0 : 2 * ROWS, :] = jnp.zeros((2 * ROWS, width), jnp.float32)
+        met_side_ref[1, 9 * ROWS : 11 * ROWS, :] = jnp.zeros((2 * ROWS, width), jnp.float32)
+        for r in range(0, 9 * ROWS, 8):
+            near, far = met_near_ref[r : r + 8, :], met_far_ref[r : r + 8, :]
+            met_side_ref[0, 2 * ROWS + r : 2 * ROWS + r + 8, :] = chosen(True, near, far)
+            met_side_ref[1, r : r + 8, :] = chosen(False, near, far)
+        for level in range(levels):
+            coefficients(level, level)
+
+        fetch.wait()
         for side in range(2):
             pltpu.matmul_push_rhs(weights_ref[side], 0, side)
         for side in range(2):
@@ -165,7 +195,6 @@
             flow = []
             for slot in range(TOGETHER):
                 level = group * TOGETHER + slot
-                coefficients(level, slot)
                 ahead = [table_ref[s * levels + level] > 0.0 for s in range(steps)]
                 way = [jnp.where(a, 1, -1).astype(jnp.int32) for a in ahead]
                 same = way[0] == way[1]
@@ -227,7 +256,7 @@
                     return base[s] + way[s] * (k + 3 * number)
 
                 def spread(at, kind):
-                    return jnp.broadcast_to(coef_ref[slot, s, pl.ds(at * 8 + kind, 1), :], (8, width))
+                    return jnp.broadcast_to(coef_ref[level, s, pl.ds(at * KINDS + kind, 1), :], (8, width))
 
                 def q(k):
                     if k not in state:
@@ -304,22 +333,44 @@
     lax.fori_loop(0, levels, level_body, 0)
 
 
-def met_kernel(groups, x_ref, y_ref, p_ref, out_ref):
-    for ref, first in ((x_ref, 0), (y_ref, 56), (p_ref, 112)):
-        count = ref.shape[0]
-        value = ref[...].reshape(count, ref.shape[2])
-        for g in range(groups):
-            out_ref[g, first : first + count, :] = value
+def met_kernel(groups, steps, x_ref, y_ref, p_ref, out_ref):
+    for s in range(steps):
+        first = s * ROWS
+        for ref in (x_ref, y_ref, p_ref):
+            count = ref.shape[0] // steps
+            value = ref[s * count : (s + 1) * count].reshape(count, ref.shape[2])
+            for g in range(groups):
+                out_ref[g, first : first + count, :] = value
+            first += count
+
+
+def block_kernel(met_ref, near_ref, far_ref):
+    odd = lax.rem(lax.axis_index("tile"), 2) == 1
+
+    def fill(above_ref, below_ref):
+        for slot, (s, g) in enumerate([(0, g) for g in range(2, 8)] + [(1, 5), (1, 6), (1, 7)]):
+            above_ref[slot * ROWS : (slot + 1) * ROWS, :] = met_ref[g, s * ROWS : (s + 1) * ROWS, :]
+        for slot, (s, g) in enumerate([(1, 0), (1, 1), (1, 2)] + [(0, g) for g in range(6)]):
+            below_ref[slot * ROWS : (slot + 1) * ROWS, :] = met_ref[g, s * ROWS : (s + 1) * ROWS, :]
+
+    @pl.when(odd)
+    def _():
+        fill(far_ref, near_ref)
+
+    @pl.when(jnp.logical_not(odd))
+    def _():
+        fill(near_ref, far_ref)
 
 
 def local(tracers, wind_x, wind_y, surface_p, coef_a, coef_b, edge_flip):
     count, levels, cells, width = tracers.shape
     steps, block = wind_x.shape[0], wind_x.shape[3]
     groups, tiles = lax.axis_size("grp"), lax.axis_size("tile")
-    stride = 120
+    stride = steps * ROWS
     smem = pl.BlockSpec(memory_space=pltpu.SMEM)
     vmem = pl.BlockSpec(memory_space=pltpu.VMEM)
     flat = (count * levels * cells, width)
+    small = pltpu.CompilerParams(vmem_limit_bytes=8 * 1024 * 1024)
     edge = jax.ShapeDtypeStruct((levels * 18 * count, width), jnp.float32)
 
     near_pairs, far_pairs = pairs(tiles)
@@ -336,15 +387,19 @@
     near = lax.ppermute(near, "tile", near_pairs)
     far = lax.ppermute(far, "tile", far_pairs)
     packed = pl.pallas_call(
-        functools.partial(met_kernel, groups),
+        functools.partial(met_kernel, groups, steps),
         out_shape=jax.ShapeDtypeStruct((groups, stride, width), jnp.float32),
         in_specs=[vmem] * 3,
         out_specs=vmem,
         name="met",
     )(wind_x.reshape(-1, 1, width), wind_y.reshape(-1, 1, width), surface_p.reshape(-1, 1, width))
     met = lax.all_to_all(packed, "grp", 0, 0, tiled=True)
-    met_near = lax.ppermute(met, "tile", near_pairs)
-    met_far = lax.ppermute(met, "tile", far_pairs)
+    part = jax.ShapeDtypeStruct((9 * ROWS, width), jnp.float32)
+    met_near, met_far = pl.pallas_call(
+        block_kernel, out_shape=(part, part), in_specs=[vmem], out_specs=(vmem, vmem), compiler_params=small, name="blocks"
+    )(met)
+    met_near = lax.ppermute(met_near, "tile", near_pairs)
+    met_far = lax.ppermute(met_far, "tile", far_pairs)
 
     met_flat = (groups * stride, width)
     dims = (steps, levels, cells, block, groups, count, stride)
@@ -355,7 +410,7 @@
             jax.ShapeDtypeStruct(flat, jnp.float32),
             jax.ShapeDtypeStruct((levels * cells, width), jnp.float32),
         ),
-        in_specs=[smem] + [vmem] * 7,
+        in_specs=[smem] + [vmem] * 6 + [pl.BlockSpec(memory_space=pl.ANY)],
         out_specs=(vmem, vmem),
         scratch_shapes=[
             pltpu.VMEM((TOGETHER, 64, count, width), jnp.float32),
@@ -363,7 +418,10 @@
             pltpu.VMEM((TOGETHER, 56, count, width), jnp.float32),
             pltpu.VMEM((TOGETHER, 40, count, width), jnp.float32),
             pltpu.VMEM((TOGETHER, 56, count, width), jnp.float32),
-            pltpu.VMEM((TOGETHER, steps, rows * 8, width), jnp.float32),
+            pltpu.VMEM((levels, steps, rows * KINDS, width), jnp.float32),
+            pltpu.VMEM((2, 11 * ROWS, width), jnp.float32),
+            pltpu.VMEM((2, 2 * width, 2 * width), jnp.bfloat16),
+            pltpu.SemaphoreType.DMA,
         ],
         compiler_params=pltpu.CompilerParams(vmem_limit_bytes=VMEM_LIMIT),
         name="advect",
@@ -373,8 +431,8 @@
         near,
         far,
         met.reshape(met_flat),
-        met_near.reshape(met_flat),
-        met_far.reshape(met_flat),
+        met_near,
+        met_far,
         jnp.asarray(stencil_weights(width)),
     )
     return out.reshape(tracers.shape), mass.reshape(levels, cells, width)

time: 47.4 us -> 46 us (0.970)
  the two profiles are of different devices: /device:TPU:4 before, /device:TPU:2 now
where the time goes in v4:
time: 46 us; the launch traced here: 45.7 us
  starting transfers between devices  19.7 us (43%)
  Pallas kernels  18.1 us (39%)
  waiting for transfers between devices  4.65 us (10%)
  local copies, waits for them, and re-layouts  2.47 us (5%)
  between operations  0.66 us (1%)
    pallas_call x1, Pallas kernels, local(): pl.pallas_call(functools.partial(advect_kernel, dims), out_shape=(jax.Sha...  13 us
    ppermute x1, starting transfers between devices, local(): far = lax.ppermute(far, 'tile', far_pairs)  6.84 us
    ppermute x1, starting transfers between devices, local(): met_far = lax.ppermute(met_far, 'tile', far_pairs)  6.82 us
    all_to_all x1, starting transfers between devices, local(): met = lax.all_to_all(packed, 'grp', 0, 0, tiled=True)  6.03 us
    ppermute x1, waiting for transfers between devices, local(): met_far = lax.ppermute(met_far, 'tile', far_pairs)  2.99 us
    pallas_call x1, Pallas kernels, local(): pl.pallas_call(functools.partial(edge_kernel, levels, cells, count), out_...  2.58 us
    all_to_all x1, waiting for transfers between devices, local(): met = lax.all_to_all(packed, 'grp', 0, 0, tiled=True)  1.65 us
    pallas_call x1, Pallas kernels, local(): pl.pallas_call(functools.partial(met_kernel, groups, steps), out_shape=ja...  1.61 us
  transfers between devices with their start and end apart: 5, of which 2 were waited for; matrix products, arithmetic and copies ran while one was open for 2% of the time, Pallas kernels for 8%

profile of v4, /device:TPU:2, one launch (start us, length us, event | category | flops | bytes accessed | tf_op | source)
XLA Modules:
  0.0 45.7 jit_solution(5808014405257770528)
XLA Ops:
  0.6 1.6 %met.1 = f32[8,128,128]{2,1,0:T(8,128)} custom-call(f32[54,1,128]{2,1,0:T(1,128)} %bitcast.10, f32[54,1,128]{2,1,0:T(1,128)} %bitcast.11, f32[6,1,128]{2,1,0:T(1,128)} %bitcast.12), custom_call_target="tpu_custom_call" | custom-call | tf_op jit(solution)/shard_map/met/pallas_call | solution.py:389
  2.2 6.0 %all-to-all-start = ((f32[8,128,128]{2,1,0:T(8,128)}), f32[8,128,128]{2,1,0:T(8,128)S(1)}, u32[]{:S(2)}, u32[]{:S(2)}) async-start(f32[8,128,128]{2,1,0:T(8,128)} %met.1), calls=%async_computation | async-start | bytes 1048576 | tf_op jit(solution)/shard_map/all_to_all | solution.py:396
  8.3 0.0 copy-start
  8.3 2.6 %edges.1 = (f32[1296,128]{1,0:T(8,128)}, f32[1296,128]{1,0:T(8,128)}) custom-call(f32[1728,128]{1,0:T(8,128)} %bitcast.8), custom_call_target="tpu_custom_call" | custom-call | tf_op jit(solution)/shard_map/edges/pallas_call | solution.py:380
  10.9 0.0 collective-permute-start
  10.9 6.8 %collective-permute-start.1 = (f32[1296,128]{1,0:T(8,128)}, f32[1296,128]{1,0:T(8,128)S(1)}, u32[]{:S(2)}, u32[]{:S(2)}) collective-permute-start(f32[1296,128]{1,0:T(8,128)} %get-tuple-element.9), channel_id=1, source_target_pairs={{0,31},{1,2},{2,1},{3,4},{4,3},{5,6},{6,5},{7,8},{8,7},{9,10},{10,... | collective-permute-start | bytes 1990664 | tf_op jit(solution)/shard_map/ppermute | solution.py:388
  17.7 1.7 %all-to-all-done.met_ref = f32[8,128,128]{2,1,0:T(8,128)S(1)} async-done(((f32[8,128,128]{2,1,0:T(8,128)}), f32[8,128,128]{2,1,0:T(8,128)S(1)}, u32[]{:S(2)}, u32[]{:S(2)}) %all-to-all-start) | async-done | bytes 524320 | tf_op jit(solution)/shard_map/all_to_all | solution.py:396
  19.4 0.9 %blocks.1 = (f32[576,128]{1,0:T(8,128)}, f32[576,128]{1,0:T(8,128)}) custom-call(f32[8,128,128]{2,1,0:T(8,128)S(1)} %all-to-all-done.met_ref), custom_call_target="tpu_custom_call" | custom-call | tf_op jit(solution)/shard_map/blocks/pallas_call | solution.py:398
  20.2 0.0 copy-start.4
  20.2 0.0 collective-permute-start.2
  20.2 6.8 %collective-permute-start.3 = (f32[576,128]{1,0:T(8,128)}, f32[576,128]{1,0:T(8,128)S(1)}, u32[]{:S(2)}, u32[]{:S(2)}) collective-permute-start(f32[576,128]{1,0:T(8,128)} %get-tuple-element.11), channel_id=1, source_target_pairs={{0,31},{1,2},{2,1},{3,4},{4,3},{5,6},{6,5},{7,8},{8,7},{9,10},{10,... | collective-permute-start | bytes 884744 | tf_op jit(solution)/shard_map/ppermute | solution.py:402
  27.0 0.0 copy-done.4
  27.1 0.9 %slice_reduce_fusion = f32[2,9]{1,0:T(2,128)S(1)} fusion(f32[2,9,1,3,128]{4,2,3,1,0:T(1,128)} %param.9), kind=kLoop, calls=%fused_computation | loop fusion | bytes 144 | tf_op jit(solution)/shard_map/slice | solution.py:378
  27.9 0.0 copy-start.2
  27.9 0.0 copy-start.3
  27.9 0.1 reshape_squeeze.3
  28.0 0.6 %copy-done.2 = f32[9]{0:T(128)S(1)} copy-done((f32[9]{0:T(128)S(1)}, f32[9]{0:T(128)}, u32[]{:S(2)}) %copy-start.2) | copy-done | bytes 60
  28.6 0.0 copy-done.3
  28.6 0.1 pad_maximum_fusion.table_ref
  28.7 0.0 collective-permute-done.near_ref
  28.7 0.0 collective-permute-done.1.far_ref
  28.7 0.0 collective-permute-done.2.met_near_ref
  28.7 3.0 %collective-permute-done.3.met_far_ref = f32[576,128]{1,0:T(8,128)S(1)} collective-permute-done((f32[576,128]{1,0:T(8,128)}, f32[576,128]{1,0:T(8,128)S(1)}, u32[]{:S(2)}, u32[]{:S(2)}) %collective-permute-start.3) | collective-permute-done | bytes 294944 | tf_op jit(solution)/shard_map/ppermute | solution.py:402
  31.7 0.0 copy-done
  31.7 0.0 copy-start.1
  31.7 0.9 %copy-done.1 = bf16[2,256,256]{2,1,0:T(8,128)(2,1)S(1)} copy-done((bf16[2,256,256]{2,1,0:T(8,128)(2,1)S(1)}, bf16[2,256,256]{2,1,0:T(8,128)(2,1)}, u32[]{:S(2)}) %copy-start.1) | copy-done | bytes 262168
  32.6 13.0 %advect.1 = (f32[1728,128]{1,0:T(8,128)}, f32[216,128]{1,0:T(8,128)}) custom-call(f32[68]{0:T(128)S(1)} %pad_maximum_fusion.table_ref, f32[1728,128]{1,0:T(8,128)S(1)} %bitcast.9, f32[1296,128]{1,0:T(8,128)S(1)} %collective-permute-done.near_ref, f32[1296,128]{1,0:T(8,128)S(1)} %collective-permute-done.1.far_ref, f32[1024,128]{1,0:T(8,128)S(1)} %bitcast.7, ...), custom_call_target="tpu_custom_call" | custom-call | tf_op jit(solution)/shard_map/advect/pallas_call | solution.py:407
  (1 shorter events, 0.0 us)
Async XLA Ops:
  2.2 17.1 %all-to-all-start = ((f32[8,128,128]{2,1,0:T(8,128)}), f32[8,128,128]{2,1,0:T(8,128)S(1)}, u32[]{:S(2)}, u32[]{:S(2)}) async-start(f32[8,128,128]{2,1,0:T(8,128)} %met.1), calls=%async_computation | async-start | bytes 1048576 | tf_op jit(solution)/shard_map/all_to_all | solution.py:396
  8.3 23.4 %copy-start = (f32[8,9,24,128]{3,2,1,0:T(8,128)S(1)}, f32[8,9,24,128]{3,2,1,0:T(8,128)}, u32[]{:S(2)}) copy-start(f32[8,9,24,128]{3,2,1,0:T(8,128)} %param.8) | copy-start | bytes 2654212
  10.9 17.8 %collective-permute-start = (f32[1296,128]{1,0:T(8,128)}, f32[1296,128]{1,0:T(8,128)S(1)}, u32[]{:S(2)}, u32[]{:S(2)}) collective-permute-start(f32[1296,128]{1,0:T(8,128)} %get-tuple-element.8), channel_id=1, source_target_pairs={{0,1},{1,0},{2,3},{3,2},{4,5},{5,4},{6,7},{7,6},{8,9},{9,8},{10,11... | collective-permute-start | bytes 1990664 | tf_op jit(solution)/shard_map/ppermute | solution.py:387
  10.9 17.8 %collective-permute-start.1 = (f32[1296,128]{1,0:T(8,128)}, f32[1296,128]{1,0:T(8,128)S(1)}, u32[]{:S(2)}, u32[]{:S(2)}) collective-permute-start(f32[1296,128]{1,0:T(8,128)} %get-tuple-element.9), channel_id=1, source_target_pairs={{0,31},{1,2},{2,1},{3,4},{4,3},{5,6},{6,5},{7,8},{8,7},{9,10},{10,... | collective-permute-start | bytes 1990664 | tf_op jit(solution)/shard_map/ppermute | solution.py:388
  20.2 6.8 %copy-start.4 = (s32[32]{0:T(128)S(1)}, s32[32]{0:T(128)}, u32[]{:S(2)}) copy-start(s32[32]{0:T(128)} %param.14) | copy-start | bytes 388
  20.2 8.4 %collective-permute-start.2 = (f32[576,128]{1,0:T(8,128)}, f32[576,128]{1,0:T(8,128)S(1)}, u32[]{:S(2)}, u32[]{:S(2)}) collective-permute-start(f32[576,128]{1,0:T(8,128)} %get-tuple-element.10), channel_id=1, source_target_pairs={{0,1},{1,0},{2,3},{3,2},{4,5},{5,4},{6,7},{7,6},{8,9},{9,8},{10,11... | collective-permute-start | bytes 884744 | tf_op jit(solution)/shard_map/ppermute | solution.py:401
  20.2 11.4 %collective-permute-start.3 = (f32[576,128]{1,0:T(8,128)}, f32[576,128]{1,0:T(8,128)S(1)}, u32[]{:S(2)}, u32[]{:S(2)}) collective-permute-start(f32[576,128]{1,0:T(8,128)} %get-tuple-element.11), channel_id=1, source_target_pairs={{0,31},{1,2},{2,1},{3,4},{4,3},{5,6},{6,5},{7,8},{8,7},{9,10},{10,... | collective-permute-start | bytes 884744 | tf_op jit(solution)/shard_map/ppermute | solution.py:402
  27.9 0.7 %copy-start.2 = (f32[9]{0:T(128)S(1)}, f32[9]{0:T(128)}, u32[]{:S(2)}) copy-start(f32[9]{0:T(128)} %param.13) | copy-start | bytes 112
  27.9 0.7 %copy-start.3 = (f32[9]{0:T(128)S(1)}, f32[9]{0:T(128)}, u32[]{:S(2)}) copy-start(f32[9]{0:T(128)} %param.12) | copy-start | bytes 112
  31.7 1.0 %copy-start.1 = (bf16[2,256,256]{2,1,0:T(8,128)(2,1)S(1)}, bf16[2,256,256]{2,1,0:T(8,128)(2,1)}, u32[]{:S(2)}) copy-start(bf16[2,256,256]{2,1,0:T(8,128)(2,1)} %constant.2.clone.weights_hbm) | copy-start | bytes 786436

commit v5 on v4

--- a/solution.py
+++ b/solution.py
@@ -318,7 +318,7 @@
     pl.run_scoped(run, *acc)
 
 
-def edge_kernel(levels, cells, tracers, field_ref, near_ref, far_ref):
+def edge_kernel(levels, cells, tracers, field_ref, table_ref, near_ref, far_ref):
     even = lax.rem(lax.axis_index("tile"), 2) == 0
     near_row = jnp.where(even, cells - 18, 0)
     far_row = cells - 18 - near_row
@@ -380,10 +380,11 @@
     near, far = pl.pallas_call(
         functools.partial(edge_kernel, levels, cells, count),
         out_shape=(edge, edge),
-        in_specs=[vmem],
+        in_specs=[vmem, pl.BlockSpec(memory_space=pl.ANY)],
         out_specs=(vmem, vmem),
+        compiler_params=small,
         name="edges",
-    )(tracers.reshape(flat))
+    )(tracers.reshape(flat), table)
     near = lax.ppermute(near, "tile", near_pairs)
     far = lax.ppermute(far, "tile", far_pairs)
     packed = pl.pallas_call(
@@ -410,7 +411,7 @@
             jax.ShapeDtypeStruct(flat, jnp.float32),
             jax.ShapeDtypeStruct((levels * cells, width), jnp.float32),
         ),
-        in_specs=[smem] + [vmem] * 6 + [pl.BlockSpec(memory_space=pl.ANY)],
+        in_specs=[smem] + [vmem] * 6 + [pl.BlockSpec(memory_space=pltpu.HBM)],
         out_specs=(vmem, vmem),
         scratch_shapes=[
             pltpu.VMEM((TOGETHER, 64, count, width), jnp.float32),

time: 46 us -> 44.4 us (0.965)
  Pallas kernels: 18.1 us -> 16.1 us
  waiting for transfers between devices: 4.65 us -> 5.67 us
  local copies, waits for them, and re-layouts: 2.47 us -> 1.53 us
    pallas_call x1, Pallas kernels: 2.58 us -> 1.34 us  [local(): pl.pallas_call(functools.partial(edge_kernel, levels, cells, count), out_...]
    ppermute x1, waiting for transfers between devices: 2.99 us -> 4.05 us  [local(): met_far = lax.ppermute(met_far, 'tile', far_pairs)]
    unnamed x10, local copies, waits for them, and re-layouts: 1.54 us -> 0.59 us
    pallas_call x1, Pallas kernels: 0.87 us -> 0.04 us  [local(): pl.pallas_call(block_kernel, out_shape=(part, part), in_specs=[vmem], out...]
  transfers between devices with their start and end apart: 5 -> 5, of which waited for: 2 -> 3; matrix products, arithmetic and copies ran while one was open for 2% -> 2% of each run, Pallas kernels for 8% -> 3%
where the time goes in v5:
time: 44.4 us; the launch traced here: 43.9 us
  starting transfers between devices  19.8 us (45%)
  Pallas kernels  16.1 us (36%)
  waiting for transfers between devices  5.67 us (13%)
  local copies, waits for them, and re-layouts  1.53 us (3%)
  between operations  0.69 us (2%)
    pallas_call x1, Pallas kernels, local(): pl.pallas_call(functools.partial(advect_kernel, dims), out_shape=(jax.Sha...  13.1 us
    ppermute x1, starting transfers between devices, local(): far = lax.ppermute(far, 'tile', far_pairs)  6.84 us
    ppermute x1, starting transfers between devices, local(): met_far = lax.ppermute(met_far, 'tile', far_pairs)  6.81 us
    all_to_all x1, starting transfers between devices, local(): met = lax.all_to_all(packed, 'grp', 0, 0, tiled=True)  6.03 us
    ppermute x1, waiting for transfers between devices, local(): met_far = lax.ppermute(met_far, 'tile', far_pairs)  4.05 us
    pallas_call x1, Pallas kernels, local(): pl.pallas_call(functools.partial(met_kernel, groups, steps), out_shape=ja...  1.69 us
    pallas_call x1, Pallas kernels, local(): pl.pallas_call(functools.partial(edge_kernel, levels, cells, count), out_...  1.34 us
    all_to_all x1, waiting for transfers between devices, local(): met = lax.all_to_all(packed, 'grp', 0, 0, tiled=True)  1.26 us
  transfers between devices with their start and end apart: 5, of which 3 were waited for; matrix products, arithmetic and copies ran while one was open for 2% of the time, Pallas kernels for 3%

profile of v5, /device:TPU:2, one launch (start us, length us, event | category | flops | bytes accessed | tf_op | source)
XLA Modules:
  0.0 43.9 jit_solution(7896578365829354036)
XLA Ops:
  0.6 0.0 copy-start
  0.6 1.7 %met.1 = f32[8,128,128]{2,1,0:T(8,128)} custom-call(f32[54,1,128]{2,1,0:T(1,128)} %bitcast.10, f32[54,1,128]{2,1,0:T(1,128)} %bitcast.11, f32[6,1,128]{2,1,0:T(1,128)} %bitcast.12), custom_call_target="tpu_custom_call" | custom-call | tf_op jit(solution)/shard_map/met/pallas_call | solution.py:390
  2.3 6.0 %all-to-all-start = ((f32[8,128,128]{2,1,0:T(8,128)}), f32[8,128,128]{2,1,0:T(8,128)S(1)}, u32[]{:S(2)}, u32[]{:S(2)}) async-start(f32[8,128,128]{2,1,0:T(8,128)} %met.1), calls=%async_computation | async-start | bytes 1048576 | tf_op jit(solution)/shard_map/all_to_all | solution.py:397
  8.4 0.0 copy-start.4
  8.4 0.9 %slice_reduce_fusion = f32[2,9]{1,0:T(2,128)S(1)} fusion(f32[2,9,1,3,128]{4,2,3,1,0:T(1,128)} %param.9), kind=kLoop, calls=%fused_computation | loop fusion | bytes 144 | tf_op jit(solution)/shard_map/slice | solution.py:378
  9.2 0.0 copy-done.4
  9.2 0.0 copy-start.2
  9.3 0.0 copy-start.3
  9.3 0.1 reshape_squeeze.3
  9.3 0.6 %copy-done.2 = f32[9]{0:T(128)S(1)} copy-done((f32[9]{0:T(128)S(1)}, f32[9]{0:T(128)}, u32[]{:S(2)}) %copy-start.2) | copy-done | bytes 60
  9.9 0.0 copy-done.3
  9.9 0.1 pad_maximum_fusion.table_ref
  10.0 0.0 copy-done
  10.0 1.3 %edges.1 = (f32[1296,128]{1,0:T(8,128)}, f32[1296,128]{1,0:T(8,128)}) custom-call(f32[1728,128]{1,0:T(8,128)S(1)} %bitcast.8, f32[68]{0:T(128)S(1)} %pad_maximum_fusion.table_ref), custom_call_target="tpu_custom_call" | custom-call | tf_op jit(solution)/shard_map/edges/pallas_call | solution.py:380
  11.3 0.0 collective-permute-start
  11.3 0.0 copy-start.1
  11.3 6.8 %collective-permute-start.1 = (f32[1296,128]{1,0:T(8,128)}, f32[1296,128]{1,0:T(8,128)S(1)}, u32[]{:S(2)}, u32[]{:S(2)}) collective-permute-start(f32[1296,128]{1,0:T(8,128)} %get-tuple-element.9), channel_id=1, source_target_pairs={{0,31},{1,2},{2,1},{3,4},{4,3},{5,6},{6,5},{7,8},{8,7},{9,10},{10,... | collective-permute-start | bytes 1990664 | tf_op jit(solution)/shard_map/ppermute | solution.py:389
  18.2 1.3 %all-to-all-done.met_ref = f32[8,128,128]{2,1,0:T(8,128)S(1)} async-done(((f32[8,128,128]{2,1,0:T(8,128)}), f32[8,128,128]{2,1,0:T(8,128)S(1)}, u32[]{:S(2)}, u32[]{:S(2)}) %all-to-all-start) | async-done | bytes 524320 | tf_op jit(solution)/shard_map/all_to_all | solution.py:397
  19.5 0.1 collective-permute-start.2
  19.6 6.8 %collective-permute-start.3 = (f32[576,128]{1,0:T(8,128)S(1)}, f32[576,128]{1,0:T(8,128)S(1)}, u32[]{:S(2)}, u32[]{:S(2)}) collective-permute-start(f32[576,128]{1,0:T(8,128)S(1)} %get-tuple-element.11), channel_id=1, source_target_pairs={{0,31},{1,2},{2,1},{3,4},{4,3},{5,6},{6,5},{7,8},{8,7},{9,10},{10,... | collective-permute-start | bytes 884744 | tf_op jit(solution)/shard_map/ppermute | solution.py:403
  26.4 0.0 collective-permute-done.near_ref
  26.4 0.3 collective-permute-done.1.far_ref
  26.7 0.0 collective-permute-done.2.met_near_ref
  26.8 4.0 %collective-permute-done.3.met_far_ref = f32[576,128]{1,0:T(8,128)S(1)} collective-permute-done((f32[576,128]{1,0:T(8,128)S(1)}, f32[576,128]{1,0:T(8,128)S(1)}, u32[]{:S(2)}, u32[]{:S(2)}) %collective-permute-start.3) | collective-permute-done | bytes 294944 | tf_op jit(solution)/shard_map/ppermute | solution.py:403
  30.8 0.0 copy-done.1
  30.8 13.1 %advect.1 = (f32[1728,128]{1,0:T(8,128)}, f32[216,128]{1,0:T(8,128)}) custom-call(f32[68]{0:T(128)S(1)} %pad_maximum_fusion.table_ref, f32[1728,128]{1,0:T(8,128)S(1)} %bitcast.9, f32[1296,128]{1,0:T(8,128)S(1)} %collective-permute-done.near_ref, f32[1296,128]{1,0:T(8,128)S(1)} %collective-permute-done.1.far_ref, f32[1024,128]{1,0:T(8,128)S(1)} %bitcast.7, ...), custom_call_target="tpu_custom_call" | custom-call | tf_op jit(solution)/shard_map/advect/pallas_call | solution.py:408
  (2 shorter events, 0.0 us)
Async XLA Ops:
  0.6 9.4 %copy-start = (f32[8,9,24,128]{3,2,1,0:T(8,128)S(1)}, f32[8,9,24,128]{3,2,1,0:T(8,128)}, u32[]{:S(2)}) copy-start(f32[8,9,24,128]{3,2,1,0:T(8,128)} %param.8) | copy-start | bytes 2654212
  2.3 17.1 %all-to-all-start = ((f32[8,128,128]{2,1,0:T(8,128)}), f32[8,128,128]{2,1,0:T(8,128)S(1)}, u32[]{:S(2)}, u32[]{:S(2)}) async-start(f32[8,128,128]{2,1,0:T(8,128)} %met.1), calls=%async_computation | async-start | bytes 1048576 | tf_op jit(solution)/shard_map/all_to_all | solution.py:397
  8.4 0.9 %copy-start.4 = (s32[32]{0:T(128)S(1)}, s32[32]{0:T(128)}, u32[]{:S(2)}) copy-start(s32[32]{0:T(128)} %param.14) | copy-start | bytes 388
  9.2 0.7 %copy-start.2 = (f32[9]{0:T(128)S(1)}, f32[9]{0:T(128)}, u32[]{:S(2)}) copy-start(f32[9]{0:T(128)} %param.13) | copy-start | bytes 112
  9.3 0.7 %copy-start.3 = (f32[9]{0:T(128)S(1)}, f32[9]{0:T(128)}, u32[]{:S(2)}) copy-start(f32[9]{0:T(128)} %param.12) | copy-start | bytes 112
  11.3 15.1 %collective-permute-start = (f32[1296,128]{1,0:T(8,128)}, f32[1296,128]{1,0:T(8,128)S(1)}, u32[]{:S(2)}, u32[]{:S(2)}) collective-permute-start(f32[1296,128]{1,0:T(8,128)} %get-tuple-element.8), channel_id=1, source_target_pairs={{0,1},{1,0},{2,3},{3,2},{4,5},{5,4},{6,7},{7,6},{8,9},{9,8},{10,11... | collective-permute-start | bytes 1990664 | tf_op jit(solution)/shard_map/ppermute | solution.py:388
  11.3 19.5 %copy-start.1 = (bf16[2,256,256]{2,1,0:T(8,128)(2,1)S(1)}, bf16[2,256,256]{2,1,0:T(8,128)(2,1)}, u32[]{:S(2)}) copy-start(bf16[2,256,256]{2,1,0:T(8,128)(2,1)} %constant.2.clone.weights_hbm) | copy-start | bytes 786436
  11.3 15.4 %collective-permute-start.1 = (f32[1296,128]{1,0:T(8,128)}, f32[1296,128]{1,0:T(8,128)S(1)}, u32[]{:S(2)}, u32[]{:S(2)}) collective-permute-start(f32[1296,128]{1,0:T(8,128)} %get-tuple-element.9), channel_id=1, source_target_pairs={{0,31},{1,2},{2,1},{3,4},{4,3},{5,6},{6,5},{7,8},{8,7},{9,10},{10,... | collective-permute-start | bytes 1990664 | tf_op jit(solution)/shard_map/ppermute | solution.py:389
  19.5 7.3 %collective-permute-start.2 = (f32[576,128]{1,0:T(8,128)S(1)}, f32[576,128]{1,0:T(8,128)S(1)}, u32[]{:S(2)}, u32[]{:S(2)}) collective-permute-start(f32[576,128]{1,0:T(8,128)S(1)} %get-tuple-element.10), channel_id=1, source_target_pairs={{0,1},{1,0},{2,3},{3,2},{4,5},{5,4},{6,7},{7,6},{8,9},{9,8},{10,11... | collective-permute-start | bytes 884744 | tf_op jit(solution)/shard_map/ppermute | solution.py:402
  19.6 11.2 %collective-permute-start.3 = (f32[576,128]{1,0:T(8,128)S(1)}, f32[576,128]{1,0:T(8,128)S(1)}, u32[]{:S(2)}, u32[]{:S(2)}) collective-permute-start(f32[576,128]{1,0:T(8,128)S(1)} %get-tuple-element.11), channel_id=1, source_target_pairs={{0,31},{1,2},{2,1},{3,4},{4,3},{5,6},{6,5},{7,8},{8,7},{9,10},{10,... | collective-permute-start | bytes 884744 | tf_op jit(solution)/shard_map/ppermute | solution.py:403

commit v6 on v5

--- a/solution.py
+++ b/solution.py
@@ -12,7 +12,7 @@
 SECTION_WEIGHTS = (1.0 / 3.0, 0.5, 1.0)
 TOGETHER = 3
 ROWS = 64
-KINDS = 7
+KINDS = 6
 SLOTS = 32
 VMEM_LIMIT = 24 * 1024 * 1024
 
@@ -24,16 +24,14 @@
 
 
 def stencil_weights(width):
-    out = np.zeros((2, 2 * width, 2 * width), np.float32)
-    for side in range(2):
-        for j in range(width):
-            face = j + side
-            for tap, value in enumerate((2.0, -13.0, 47.0, 27.0, -3.0)):
-                up = min(max(face - 3 + tap, 0), width - 1)
-                down = min(max(face + 2 - tap, 0), width - 1)
-                for half in (0, width):
-                    out[side, half + up, j] += value
-                    out[side, half + down, width + j] += value
+    out = np.zeros((2 * width, 2 * width), np.float32)
+    for j in range(width):
+        for tap, value in enumerate((2.0, -13.0, 47.0, 27.0, -3.0)):
+            up = min(max(j - 3 + tap, 0), width - 1)
+            down = min(max(j + 2 - tap, 0), width - 1)
+            for half in (0, width):
+                out[half + up, j] += value
+                out[half + down, width + j] += value
     return out.astype(ml_dtypes.bfloat16)
 
 
@@ -162,7 +160,7 @@
                             after = jnp.where(last_row, pltpu.roll(face_x[t + 1][0], groups - 1, 0), after)
                     face_y, next_y = faces_y[t][c]
                     div = (after - face_x[t][c]) + (next_y - face_y)
-                    kinds = [jnp.abs(face_x[t][c]) * (1.0 / 30.0), face_y * (1.0 / 60.0), next_y * (1.0 / 60.0)]
+                    kinds = [jnp.abs(face_x[t][c]) * (1.0 / 30.0), face_y * (1.0 / 60.0)]
                     for weight in SECTION_WEIGHTS:
                         kinds.append(weight / (mass[t][c] - weight * div))
                     kinds.append(mass[t][c])
@@ -186,7 +184,7 @@
 
         fetch.wait()
         for side in range(2):
-            pltpu.matmul_push_rhs(weights_ref[side], 0, side)
+            pltpu.matmul_push_rhs(weights_ref[...], 0, side)
         for side in range(2):
             pltpu.matmul_acc_lhs(accs[side], jnp.zeros((16, 256), jnp.bfloat16), load_staged_rhs=0)
             out_ref[0:16, :] = pltpu.matmul_pop(accs[side])[:, :width]
@@ -234,10 +232,8 @@
                 high = both.astype(jnp.bfloat16)
                 rest = (both - high.astype(jnp.float32)).astype(jnp.bfloat16)
                 lhs = jnp.concatenate([high, rest], axis=1)
-                place = pushed[0] % SLOTS
+                pltpu.matmul_acc_lhs(accs[pushed[0] % SLOTS], lhs)
                 pushed[0] += 1
-                for side in range(2):
-                    pltpu.matmul_acc_lhs(accs[2 * place + side], lhs)
 
             state = {}
 
@@ -246,9 +242,8 @@
                 s, number, source, pad, target = plan[n]
                 level, ahead, way, same, base = flow[slot]
                 weight = SECTION_WEIGHTS[number]
-                place = popped[0] % SLOTS
+                pops = pltpu.matmul_pop(accs[popped[0] % SLOTS])
                 popped[0] += 1
-                pops = [pltpu.matmul_pop(accs[2 * place + side]) for side in range(2)]
                 if part == 0:
                     state.clear()
 
@@ -276,20 +271,18 @@
                         continue
                     at = spot(k)
                     after = along_x(k + 1)
-                    sides = []
-                    for side in range(2):
-                        flux = spread(at, 1 + side)
-                        rows_of = pops[side][8 * half : 8 * half + 8]
-                        sides.append(flux * jnp.where(flux >= 0.0, rows_of[:, :width], rows_of[:, width:]))
-                    div = (after - state["before"]) + (sides[1] - sides[0])
+                    flux = spread(at, 1)
+                    faces = pops[8 * half : 8 * half + 8]
+                    along_y = flux * jnp.where(flux >= 0.0, faces[:, :width], faces[:, width:])
+                    div = (after - state["before"]) + (shift(along_y, -1) - along_y)
                     if number == 0:
-                        start = q(k + 3) * spread(at, 6)
+                        start = q(k + 3) * spread(at, 5)
                         start_ref[slot, k] = start
                     else:
                         start = start_ref[slot, k + 3 * number]
                     if weight != 1.0:
                         start = start * (1.0 / weight)
-                    value = (start - div) * spread(at, 3 + number)
+                    value = (start - div) * spread(at, 2 + number)
                     if target is None:
                         i = jnp.where(ahead[1], k, cells - 1 - k)
                         out_ref[pl.ds(level * cells + i, tracers, stride=levels * cells), :] = value
@@ -314,7 +307,7 @@
 
         lax.fori_loop(0, levels // TOGETHER, group_body, 0)
 
-    acc = [pltpu.ACC(side)((16, 256), jnp.float32) for _ in range(SLOTS) for side in range(2)]
+    acc = [pltpu.ACC(place % 2)((16, 256), jnp.float32) for place in range(SLOTS)]
     pl.run_scoped(run, *acc)
 
 
@@ -421,7 +414,7 @@
             pltpu.VMEM((TOGETHER, 56, count, width), jnp.float32),
             pltpu.VMEM((levels, steps, rows * KINDS, width), jnp.float32),
             pltpu.VMEM((2, 11 * ROWS, width), jnp.float32),
-            pltpu.VMEM((2, 2 * width, 2 * width), jnp.bfloat16),
+            pltpu.VMEM((2 * width, 2 * width), jnp.bfloat16),
             pltpu.SemaphoreType.DMA,
         ],
         compiler_params=pltpu.CompilerParams(vmem_limit_bytes=VMEM_LIMIT),

time: 44.4 us -> 44 us (level)
  transfers between devices with their start and end apart: 5 -> 5, of which waited for: 3 -> 2; matrix products, arithmetic and copies ran while one was open for 2% -> 2% of each run, Pallas kernels for 3% -> 3%
where the time goes in v6:
time: 44 us; the launch traced here: 43.7 us
  starting transfers between devices  19.8 us (45%)
  Pallas kernels  15.8 us (36%)
  waiting for transfers between devices  5.89 us (13%)
  local copies, waits for them, and re-layouts  1.53 us (3%)
  between operations  0.69 us (2%)
    pallas_call x1, Pallas kernels, local(): pl.pallas_call(functools.partial(advect_kernel, dims), out_shape=(jax.Sha...  12.9 us
    ppermute x1, starting transfers between devices, local(): far = lax.ppermute(far, 'tile', far_pairs)  6.84 us
    ppermute x1, starting transfers between devices, local(): met_far = lax.ppermute(met_far, 'tile', far_pairs)  6.81 us
    all_to_all x1, starting transfers between devices, local(): met = lax.all_to_all(packed, 'grp', 0, 0, tiled=True)  6.03 us
    ppermute x1, waiting for transfers between devices, local(): met_far = lax.ppermute(met_far, 'tile', far_pairs)  4.39 us
    pallas_call x1, Pallas kernels, local(): pl.pallas_call(functools.partial(met_kernel, groups, steps), out_shape=ja...  1.68 us
    all_to_all x1, waiting for transfers between devices, local(): met = lax.all_to_all(packed, 'grp', 0, 0, tiled=True)  1.49 us
    pallas_call x1, Pallas kernels, local(): pl.pallas_call(functools.partial(edge_kernel, levels, cells, count), out_...  1.12 us
  transfers between devices with their start and end apart: 5, of which 2 were waited for; matrix products, arithmetic and copies ran while one was open for 2% of the time, Pallas kernels for 3%

profile of v6, /device:TPU:2, one launch (start us, length us, event | category | flops | bytes accessed | tf_op | source)
XLA Modules:
  0.0 43.7 jit_solution(10173507693892124491)
XLA Ops:
  0.6 0.0 copy-start
  0.6 1.7 %met.1 = f32[8,128,128]{2,1,0:T(8,128)} custom-call(f32[54,1,128]{2,1,0:T(1,128)} %bitcast.10, f32[54,1,128]{2,1,0:T(1,128)} %bitcast.11, f32[6,1,128]{2,1,0:T(1,128)} %bitcast.12), custom_call_target="tpu_custom_call" | custom-call | tf_op jit(solution)/shard_map/met/pallas_call | solution.py:383
  2.3 6.0 %all-to-all-start = ((f32[8,128,128]{2,1,0:T(8,128)}), f32[8,128,128]{2,1,0:T(8,128)S(1)}, u32[]{:S(2)}, u32[]{:S(2)}) async-start(f32[8,128,128]{2,1,0:T(8,128)} %met.1), calls=%async_computation | async-start | bytes 1048576 | tf_op jit(solution)/shard_map/all_to_all | solution.py:390
  8.4 0.0 copy-start.4
  8.4 0.9 %slice_reduce_fusion = f32[2,9]{1,0:T(2,128)S(1)} fusion(f32[2,9,1,3,128]{4,2,3,1,0:T(1,128)} %param.9), kind=kLoop, calls=%fused_computation | loop fusion | bytes 144 | tf_op jit(solution)/shard_map/slice | solution.py:371
  9.2 0.0 copy-done.4
  9.2 0.0 copy-start.2
  9.2 0.0 copy-start.3
  9.3 0.1 reshape_squeeze.3
  9.3 0.6 %copy-done.2 = f32[9]{0:T(128)S(1)} copy-done((f32[9]{0:T(128)S(1)}, f32[9]{0:T(128)}, u32[]{:S(2)}) %copy-start.2) | copy-done | bytes 60
  9.9 0.0 copy-done.3
  9.9 0.1 pad_maximum_fusion.table_ref
  10.0 0.0 copy-done
  10.0 1.1 %edges.1 = (f32[1296,128]{1,0:T(8,128)}, f32[1296,128]{1,0:T(8,128)S(1)}) custom-call(f32[1728,128]{1,0:T(8,128)S(1)} %bitcast.8, f32[68]{0:T(128)S(1)} %pad_maximum_fusion.table_ref), custom_call_target="tpu_custom_call" | custom-call | tf_op jit(solution)/shard_map/edges/pallas_call | solution.py:373
  11.1 0.0 collective-permute-start
  11.1 0.0 copy-start.1
  11.1 6.8 %collective-permute-start.1 = (f32[1296,128]{1,0:T(8,128)S(1)}, f32[1296,128]{1,0:T(8,128)S(1)}, u32[]{:S(2)}, u32[]{:S(2)}) collective-permute-start(f32[1296,128]{1,0:T(8,128)S(1)} %get-tuple-element.9), channel_id=1, source_target_pairs={{0,31},{1,2},{2,1},{3,4},{4,3},{5,6},{6,5},{7,8},{8,7},{9,10},{10,... | collective-permute-start | bytes 1990664 | tf_op jit(solution)/shard_map/ppermute | solution.py:382
  18.0 1.5 %all-to-all-done.met_ref = f32[8,128,128]{2,1,0:T(8,128)S(1)} async-done(((f32[8,128,128]{2,1,0:T(8,128)}), f32[8,128,128]{2,1,0:T(8,128)S(1)}, u32[]{:S(2)}, u32[]{:S(2)}) %all-to-all-start) | async-done | bytes 524320 | tf_op jit(solution)/shard_map/all_to_all | solution.py:390
  19.5 0.1 collective-permute-start.2
  19.6 6.8 %collective-permute-start.3 = (f32[576,128]{1,0:T(8,128)S(1)}, f32[576,128]{1,0:T(8,128)S(1)}, u32[]{:S(2)}, u32[]{:S(2)}) collective-permute-start(f32[576,128]{1,0:T(8,128)S(1)} %get-tuple-element.11), channel_id=1, source_target_pairs={{0,31},{1,2},{2,1},{3,4},{4,3},{5,6},{6,5},{7,8},{8,7},{9,10},{10,... | collective-permute-start | bytes 884744 | tf_op jit(solution)/shard_map/ppermute | solution.py:396
  26.4 0.0 collective-permute-done.near_ref
  26.4 0.0 collective-permute-done.1.far_ref
  26.4 0.0 collective-permute-done.2.met_near_ref
  26.4 4.4 %collective-permute-done.3.met_far_ref = f32[576,128]{1,0:T(8,128)S(1)} collective-permute-done((f32[576,128]{1,0:T(8,128)S(1)}, f32[576,128]{1,0:T(8,128)S(1)}, u32[]{:S(2)}, u32[]{:S(2)}) %collective-permute-start.3) | collective-permute-done | bytes 294944 | tf_op jit(solution)/shard_map/ppermute | solution.py:396
  30.8 0.0 copy-done.1
  30.8 12.9 %advect.1 = (f32[1728,128]{1,0:T(8,128)}, f32[216,128]{1,0:T(8,128)}) custom-call(f32[68]{0:T(128)S(1)} %pad_maximum_fusion.table_ref, f32[1728,128]{1,0:T(8,128)S(1)} %bitcast.9, f32[1296,128]{1,0:T(8,128)S(1)} %collective-permute-done.near_ref, f32[1296,128]{1,0:T(8,128)S(1)} %collective-permute-done.1.far_ref, f32[1024,128]{1,0:T(8,128)S(1)} %bitcast.7, ...), custom_call_target="tpu_custom_call" | custom-call | tf_op jit(solution)/shard_map/advect/pallas_call | solution.py:401
  (2 shorter events, 0.0 us)
Async XLA Ops:
  0.6 9.4 %copy-start = (f32[8,9,24,128]{3,2,1,0:T(8,128)S(1)}, f32[8,9,24,128]{3,2,1,0:T(8,128)}, u32[]{:S(2)}) copy-start(f32[8,9,24,128]{3,2,1,0:T(8,128)} %param.8) | copy-start | bytes 2654212
  2.3 17.1 %all-to-all-start = ((f32[8,128,128]{2,1,0:T(8,128)}), f32[8,128,128]{2,1,0:T(8,128)S(1)}, u32[]{:S(2)}, u32[]{:S(2)}) async-start(f32[8,128,128]{2,1,0:T(8,128)} %met.1), calls=%async_computation | async-start | bytes 1048576 | tf_op jit(solution)/shard_map/all_to_all | solution.py:390
  8.4 0.9 %copy-start.4 = (s32[32]{0:T(128)S(1)}, s32[32]{0:T(128)}, u32[]{:S(2)}) copy-start(s32[32]{0:T(128)} %param.14) | copy-start | bytes 388
  9.2 0.7 %copy-start.2 = (f32[9]{0:T(128)S(1)}, f32[9]{0:T(128)}, u32[]{:S(2)}) copy-start(f32[9]{0:T(128)} %param.13) | copy-start | bytes 112
  9.2 0.7 %copy-start.3 = (f32[9]{0:T(128)S(1)}, f32[9]{0:T(128)}, u32[]{:S(2)}) copy-start(f32[9]{0:T(128)} %param.12) | copy-start | bytes 112
  11.1 15.3 %collective-permute-start = (f32[1296,128]{1,0:T(8,128)}, f32[1296,128]{1,0:T(8,128)S(1)}, u32[]{:S(2)}, u32[]{:S(2)}) collective-permute-start(f32[1296,128]{1,0:T(8,128)} %get-tuple-element.8), channel_id=1, source_target_pairs={{0,1},{1,0},{2,3},{3,2},{4,5},{5,4},{6,7},{7,6},{8,9},{9,8},{10,11... | collective-permute-start | bytes 1990664 | tf_op jit(solution)/shard_map/ppermute | solution.py:381
  11.1 19.7 %copy-start.1 = (bf16[256,256]{1,0:T(8,128)(2,1)S(1)}, bf16[256,256]{1,0:T(8,128)(2,1)}, u32[]{:S(2)}) copy-start(bf16[256,256]{1,0:T(8,128)(2,1)} %constant.2.clone.weights_hbm) | copy-start | bytes 393220
  11.1 15.3 %collective-permute-start.1 = (f32[1296,128]{1,0:T(8,128)S(1)}, f32[1296,128]{1,0:T(8,128)S(1)}, u32[]{:S(2)}, u32[]{:S(2)}) collective-permute-start(f32[1296,128]{1,0:T(8,128)S(1)} %get-tuple-element.9), channel_id=1, source_target_pairs={{0,31},{1,2},{2,1},{3,4},{4,3},{5,6},{6,5},{7,8},{8,7},{9,10},{10,... | collective-permute-start | bytes 1990664 | tf_op jit(solution)/shard_map/ppermute | solution.py:382
  19.5 6.9 %collective-permute-start.2 = (f32[576,128]{1,0:T(8,128)S(1)}, f32[576,128]{1,0:T(8,128)S(1)}, u32[]{:S(2)}, u32[]{:S(2)}) collective-permute-start(f32[576,128]{1,0:T(8,128)S(1)} %get-tuple-element.10), channel_id=1, source_target_pairs={{0,1},{1,0},{2,3},{3,2},{4,5},{5,4},{6,7},{7,6},{8,9},{9,8},{10,11... | collective-permute-start | bytes 884744 | tf_op jit(solution)/shard_map/ppermute | solution.py:395
  19.6 11.2 %collective-permute-start.3 = (f32[576,128]{1,0:T(8,128)S(1)}, f32[576,128]{1,0:T(8,128)S(1)}, u32[]{:S(2)}, u32[]{:S(2)}) collective-permute-start(f32[576,128]{1,0:T(8,128)S(1)} %get-tuple-element.11), channel_id=1, source_target_pairs={{0,31},{1,2},{2,1},{3,4},{4,3},{5,6},{6,5},{7,8},{8,7},{9,10},{10,... | collective-permute-start | bytes 884744 | tf_op jit(solution)/shard_map/ppermute | solution.py:396
